TPU v7x, 128 devices: a whole 4x4x4 slice. The times are simulated.
128 devices in a mesh: row: 16 (over z, y), col: 8 (over x, core).
Axes of the slice: x: 4, y: 4, z: 4, core: 2. Of those that a mesh axis runs over, the one named last changes fastest.
Arguments:
- struct_disp: float32 [48, 32768], P(None, ('row', 'col')), may hold values from -6 to 6
- target: int32 [32768], P(('row', 'col')), may hold values from 0 to 32767, as said below
- inverse: bfloat16 [32768, 32768], P('row', 'col'), may hold values from -0.046875 to 0.046875
- centre_xyz: float32 [3, 32768], replicated, may hold values from 0 to 1, as said below
- node_xyz: float32 [3, 262144], P(None, ('row', 'col')), may hold values from 0 to 1, as said below
Outputs:
- volume_disp: float32 [48, 262144], P(None, ('row', 'col'))
Inputs may be any that keep to these rules, and one draw needn't show every extreme that they name: `target`: centre j is held by the owner of index r * 8 + c with c = j // 4096 and r = (j % 4096) // 256. The 256 entries of one device name centres of at most 4 entries for any one owner, and one owner receives exactly 4 entries from every device. `centre_xyz`: every centre lies on the boundary of the cube that spans 0.3 to 0.7 in each coordinate. `node_xyz`: every volume node lies outside the cube that spans 0.3 to 0.7 in each coordinate, or on its boundary.
All inputs are finite; a program needn't handle non-finite values.
Results may differ from a plain program's by a relative error of at most 0.0049.
Values may be sent and summed in bfloat16 or wider, within the bound.
No kernel may reach another device: no remote copies, remote signals or barrier semaphores. Data moves between devices by JAX's collectives and lax.ppermute only.
A program may use at most 64 MiB of HBM per device.

v0:
```python
import math

import jax
import jax.numpy as jnp
from jax import lax
from jax.experimental import pallas as pl
from jax.experimental.pallas import tpu as pltpu
from jax.sharding import PartitionSpec as P

M = 32768
CAP = 4
RADIUS = 2.0 / math.sqrt(M)
SCALE = 4.0 / RADIUS
GROUP = 8
BATCH = 32
LANES = 128
BLOCK = 32
BOX = 16
FACES = (
    (1, 0, (0, 0, 0), 0),
    (2, 0, (1, 0, 0), 0),
    (0, 0, (0, 0, 0), 1),
    (1, 1, (0, 1, 0), 0),
    (0, 1, (1, 1, 0), 2),
    (2, 1, (1, 1, 1), 0),
)


def exchange(value, axes):
    return lax.all_to_all(value, axes, split_axis=0, concat_axis=0, tiled=True)


def routed_entries(struct_disp, target, rows, cols, col_block):
    disp_rows, entries = struct_disp.shape
    owner_block = col_block // rows
    owner_col = target // col_block
    owner_row = target % col_block // owner_block
    offsets = target % owner_block
    owner = owner_row * cols + owner_col
    position = jnp.arange(entries, dtype=jnp.int32)
    earlier = (owner[:, None] == owner[None, :]) & (position[:, None] < position[None, :])
    rank = jnp.sum(earlier.astype(jnp.int32), axis=0)
    slots = rows * CAP
    slot = owner_col * slots + owner_row * CAP + rank
    pick = (jnp.arange(cols * slots, dtype=jnp.int32)[:, None] == slot[None, :]).astype(jnp.bfloat16)
    payload = jnp.concatenate(
        [
            struct_disp.astype(jnp.bfloat16),
            offsets.astype(jnp.bfloat16)[None, :],
            jnp.zeros((64 - disp_rows - 1, entries), jnp.bfloat16),
        ],
        axis=0,
    )
    packed = lax.dot_general(
        pick, payload, (((1,), (1,)), ((), ())), preferred_element_type=jnp.float32
    ).astype(jnp.bfloat16)
    packed = packed.reshape(cols, slots, 64)
    half = slots // 2
    packed = jnp.concatenate([packed[:, :half], packed[:, half:]], axis=-1)
    return jnp.broadcast_to(packed[None], (rows, cols, half, 128)).reshape(rows * cols, half, 128)


def column_displacements(recv, disp_rows, rows, cols, col_block):
    owner_block = col_block // rows
    recv = recv.reshape(rows * cols, rows // 2, CAP, 128).transpose(1, 0, 2, 3)
    recv = recv.reshape(rows // 2, rows * cols * CAP, 128)
    columns = jnp.arange(owner_block, dtype=jnp.int32).astype(jnp.bfloat16)
    halves = []
    for side in range(2):
        part = recv[:, :, side * 64 : side * 64 + 64]
        place = (part[:, :, disp_rows : disp_rows + 1] == columns[None, None, :]).astype(jnp.bfloat16)
        halves.append(
            lax.dot_general(
                part[:, :, :disp_rows],
                place,
                (((1,), (1,)), ((0,), (0,))),
                preferred_element_type=jnp.float32,
            )
        )
    summed = jnp.concatenate(halves, axis=0).astype(jnp.bfloat16)
    return summed.transpose(1, 0, 2).reshape(disp_rows, col_block)


def surface_key(xyz):
    bits = 6
    side = 1 << bits
    offset = xyz - 0.5
    size = jnp.abs(offset)
    on_x = (size[0] >= size[1]) & (size[0] >= size[2])
    on_y = jnp.logical_not(on_x) & (size[1] >= size[2])
    normal = jnp.where(on_x, offset[0], jnp.where(on_y, offset[1], offset[2]))
    face = jnp.where(on_x, 0, jnp.where(on_y, 1, 2)) * 2 + (normal > 0).astype(jnp.int32)
    cell = jnp.clip((side * (xyz - 0.3) / 0.4).astype(jnp.int32), 0, side - 1)
    code, u, v = [jnp.zeros_like(face) for _ in range(3)]
    for place, (axis, sign, corner, first) in enumerate(FACES):
        here = face == 2 * axis + sign
        second = 3 - axis - first
        along = [side - 1 - cell[w] if corner[w] else cell[w] for w in (first, second)]
        code = jnp.where(here, place * side * side, code)
        u = jnp.where(here, along[0], u)
        v = jnp.where(here, along[1], v)
    for bit in reversed(range(bits)):
        step = 1 << bit
        u_on = (u >> bit) & 1
        v_on = (v >> bit) & 1
        code = code + step * step * ((3 * u_on) ^ v_on)
        flip = (v_on == 0) & (u_on == 1)
        u, v = jnp.where(flip, side - 1 - u, u), jnp.where(flip, side - 1 - v, v)
        u, v = jnp.where(v_on == 0, v, u), jnp.where(v_on == 0, u, v)
    return code


def sorted_rank(xyz):
    count = xyz.shape[1]
    key = surface_key(xyz) * count + jnp.arange(count, dtype=jnp.int32)
    return jnp.sum((key[:, None] < key[None, :]).astype(jnp.int32), axis=0)


def pick_columns(xyz, pick):
    high = lax.reduce_precision(xyz, 8, 7)
    middle = lax.reduce_precision(xyz - high, 8, 7)
    low = xyz - high - middle
    parts = jnp.concatenate([high, middle, low], axis=0).astype(jnp.bfloat16)
    picked = jnp.dot(parts, pick, preferred_element_type=jnp.float32)
    return picked[0:3] + picked[3:6] + picked[6:9]


def with_boxes(xyz, size):
    count = xyz.shape[1]
    runs = xyz.reshape(3, count // size, size)
    boxes = jnp.concatenate([jnp.min(runs, axis=2), jnp.max(runs, axis=2)], axis=0).reshape(-1)
    row = jnp.pad(boxes, (0, count - boxes.shape[0]))
    return jnp.concatenate([xyz, row[None, :]], axis=0)


def near_groups(centre_data, node_data):
    rows, _, piece = centre_data.shape
    cols, _, nodes = node_data.shape
    boxes = piece // BOX
    groups = nodes // GROUP
    total = cols * groups
    turns = LANES // BLOCK
    centre_box = centre_data[:, 3, : 6 * boxes].reshape(rows, 6, boxes)
    node_box = node_data[:, 3, : 6 * groups].reshape(cols, 6, groups).transpose(1, 0, 2).reshape(6, total)
    apart = jnp.zeros((rows, boxes, total), jnp.float32)
    for axis in range(3):
        low = centre_box[:, axis, :, None] - node_box[None, None, 3 + axis, :]
        high = node_box[None, None, axis, :] - centre_box[:, 3 + axis, :, None]
        gap = jnp.maximum(jnp.maximum(low, high), 0.0)
        apart = apart + gap * gap
    apart = apart.reshape(rows // turns, turns, piece // LANES, turns, BLOCK // BOX, total)
    apart = jnp.min(apart, axis=(0, 4))
    turned = [jnp.roll(apart[k], -k, axis=1) for k in range(turns)]
    apart = jnp.minimum(jnp.minimum(turned[0], turned[1]), jnp.minimum(turned[2], turned[3]))
    near = apart.reshape(piece // BLOCK, total) <= RADIUS * RADIUS * 1.001
    blocks = near.shape[0]
    spans = total // LANES
    ones = near.astype(jnp.bfloat16).reshape(blocks * spans, LANES)
    lane = jnp.arange(LANES)
    upto = (lane[:, None] <= lane[None, :]).astype(jnp.bfloat16)
    within = jnp.dot(ones, upto, preferred_element_type=jnp.float32).reshape(blocks, spans, LANES)
    span_count = within[:, :, -1]
    span = jnp.arange(spans)
    ahead = jnp.sum(
        jnp.where(span[None, :, None] < span[None, None, :], span_count[:, :, None], 0.0), axis=1
    )
    place = (within + ahead[:, :, None]).reshape(blocks, total).astype(jnp.int32) - 1
    counts = place[:, -1] + 1
    place = jnp.where(near, place, -1)
    number = jnp.arange(total, dtype=jnp.int32)
    major = (place[:, :, None] // LANES == span[None, None, :]) & near[:, :, None]
    minor = place[:, :, None] % LANES == lane[None, None, :]
    digits = [jnp.where(minor, d[None, :, None], 0).astype(jnp.bfloat16) for d in (number // 64, number % 64)]
    listed = lax.dot_general(
        major.astype(jnp.bfloat16),
        jnp.concatenate(digits, axis=2),
        (((1,), (1,)), ((0,), (0,))),
        preferred_element_type=jnp.float32,
    )
    listed = (listed[:, :, :LANES] * 64.0 + listed[:, :, LANES:]).reshape(blocks, total)
    listed = jnp.pad(listed.astype(jnp.int32), ((0, 0), (0, BATCH)))
    slots = jnp.arange(total + BATCH, dtype=jnp.int32)
    return counts, jnp.where(slots[None, :] < counts[:, None], listed, total)


def interpolate(counts, lists, node_data, centre_data, coefs):
    rows, disp_rows, piece = coefs.shape
    cols, _, nodes = node_data.shape
    total = cols * nodes
    turns = LANES // BLOCK
    quads = rows // turns

    def kernel(count_ref, list_ref, node_ref, centre_ref, coef_ref, out_ref, acc_ref, row_ref, place_ref, weight_ref):
        acc_ref[total:, :] = jnp.zeros((GROUP, LANES), jnp.float32)
        for col in range(cols):

            def prepare(step, carry):
                first = pl.multiple_of(step * LANES, LANES)
                flat = node_ref[col, :, pl.ds(first, LANES)] * SCALE
                flat = jnp.concatenate([flat, flat], axis=0)
                row_ref[pl.ds(col * nodes + first, LANES), :] = flat.T
                acc_ref[pl.ds(col * nodes + first, LANES), :] = jnp.zeros((LANES, LANES), jnp.float32)
                return carry

            lax.fori_loop(0, nodes // LANES, prepare, 0)

        lane = lax.broadcasted_iota(jnp.int32, (1, LANES), 1)
        segment = lane // BLOCK

        def gather(take, block):
            value = take((-block) % turns)
            for k in range(1, turns):
                value = jnp.where(segment == k, take((k - block) % turns), value)
            return value

        for block in range(piece // BLOCK):
            lanes = slice(block // turns * LANES, (block // turns + 1) * LANES)
            for quad in range(quads):
                coef = gather(lambda k: coef_ref[turns * quad + k, :, lanes].astype(jnp.float32), block)
                weight_ref[:, quad * LANES : (quad + 1) * LANES] = coef.astype(jnp.bfloat16)
                for axis in range(3):
                    centre = gather(lambda k: centre_ref[turns * quad + k, axis : axis + 1, lanes], block)
                    place_ref[3 * quad + axis : 3 * quad + axis + 1, :] = centre * SCALE

            def batch(step, carry):
                ids = [list_ref[block, step * BATCH + i] for i in range(BATCH)]
                node = jnp.concatenate(
                    [
                        row_ref[pl.ds(pl.multiple_of(jnp.minimum(i, total // GROUP - 1) * GROUP, GROUP), GROUP), :]
                        for i in ids
                    ],
                    axis=0,
                )
                node = [jnp.broadcast_to(node[:, a : a + 1], (GROUP * BATCH, LANES)) for a in range(3)]
                part = jnp.zeros((GROUP * BATCH, disp_rows), jnp.float32)
                for pair in range(quads // 2):
                    tiles = []
                    for quad in (2 * pair, 2 * pair + 1):
                        squared = None
                        for axis in range(3):
                            difference = node[axis] - place_ref[3 * quad + axis : 3 * quad + axis + 1, :]
                            square = difference * difference
                            squared = square if squared is None else squared + square
                        scaled = squared * lax.rsqrt(jnp.maximum(squared, 1e-30))
                        remain = jnp.maximum(4.0 - scaled, 0.0)
                        remain = remain * remain
                        tiles.append((remain * remain * (scaled + 1.0)).astype(jnp.bfloat16))
                    part = part + lax.dot_general(
                        jnp.concatenate(tiles, axis=1),
                        weight_ref[:, pair * 2 * LANES : (pair + 1) * 2 * LANES],
                        (((1,), (1,)), ((), ())),
                        preferred_element_type=jnp.float32,
                    )
                for i, number in enumerate(ids):
                    start = pl.multiple_of(number * GROUP, GROUP)
                    acc_ref[pl.ds(start, GROUP), :disp_rows] += part[i * GROUP : (i + 1) * GROUP]
                return carry

            lax.fori_loop(0, (count_ref[block] + BATCH - 1) // BATCH, batch, 0)

        low_lanes = lane < LANES // 2
        for col in range(cols):

            def pack(step, carry):
                first = pl.multiple_of(step * LANES, LANES)
                low = acc_ref[pl.ds(col * nodes + first, LANES), :]
                high = acc_ref[pl.ds(col * nodes + nodes // 2 + first, LANES), :]
                both = jnp.where(low_lanes, low, pltpu.roll(high, LANES // 2, 1))
                out_ref[col, pl.ds(first, LANES), :] = (both * (1.0 / 256.0)).astype(jnp.bfloat16)
                return carry

            lax.fori_loop(0, nodes // 2 // LANES, pack, 0)

    vmem = pl.BlockSpec(memory_space=pltpu.VMEM)
    smem = pl.BlockSpec(memory_space=pltpu.SMEM)
    return pl.pallas_call(
        kernel,
        out_shape=jax.ShapeDtypeStruct((cols, nodes // 2, LANES), jnp.bfloat16),
        in_specs=[smem, smem, vmem, vmem, vmem],
        out_specs=vmem,
        scratch_shapes=[
            pltpu.VMEM((total + GROUP, LANES), jnp.float32),
            pltpu.VMEM((total, 8), jnp.float32),
            pltpu.VMEM((16, LANES), jnp.float32),
            pltpu.VMEM((disp_rows, quads * LANES), jnp.bfloat16),
        ],
        name="interpolate",
    )(counts, lists, node_data, centre_data, coefs)


def per_device(struct_disp, target, inverse, centre_xyz, node_xyz):
    rows = lax.axis_size("row")
    cols = lax.axis_size("col")
    row_block, col_block = inverse.shape
    disp_rows = struct_disp.shape[0]
    nodes = node_xyz.shape[1]
    piece = row_block // cols
    row_index = lax.axis_index("row")

    send = routed_entries(struct_disp, target, rows, cols, col_block)
    own_xyz = lax.dynamic_slice_in_dim(centre_xyz, row_index * row_block, row_block, 1)
    send, own_xyz, node_xyz = lax.optimization_barrier((send, own_xyz, node_xyz))
    recv = exchange(send, ("row", "col"))

    rank = sorted_rank(own_xyz)
    turn = (rank // BLOCK + row_index) % (LANES // BLOCK)
    centre_slot = rank // LANES * LANES + turn * BLOCK + rank % BLOCK
    order = jnp.arange(row_block, dtype=jnp.int32)
    centre_pick = (centre_slot[:, None] == order[None, :]).astype(jnp.bfloat16)
    piece_order = lax.axis_index("col") * piece + jnp.arange(piece, dtype=jnp.int32)
    piece_pick = (centre_slot[:, None] == piece_order[None, :]).astype(jnp.bfloat16)
    piece_data = with_boxes(pick_columns(own_xyz, piece_pick), BOX)
    centre_data = exchange(jnp.broadcast_to(piece_data[None], (rows, 4, piece)), "row")

    node_rank = sorted_rank(node_xyz)
    node_order = jnp.arange(nodes, dtype=jnp.int32)
    node_pick = (node_rank[:, None] == node_order[None, :]).astype(jnp.bfloat16)
    own_nodes = with_boxes(pick_columns(node_xyz, node_pick), GROUP)
    node_data = exchange(jnp.broadcast_to(own_nodes[None], (cols, 4, nodes)), "col")
    counts, lists = near_groups(centre_data, node_data)

    disp_bf = column_displacements(recv, disp_rows, rows, cols, col_block)
    partial = lax.dot_general(
        disp_bf, inverse, (((1,), (1,)), ((), ())), preferred_element_type=jnp.float32
    )
    partial = jnp.dot(partial.astype(jnp.bfloat16), centre_pick, preferred_element_type=jnp.float32)
    partial = partial.astype(jnp.bfloat16).reshape(disp_rows, cols, piece).transpose(1, 0, 2)
    coef = jnp.sum(exchange(partial, "col").astype(jnp.float32), axis=0)
    coef = lax.optimization_barrier(coef).astype(jnp.bfloat16)
    coefs = exchange(jnp.broadcast_to(coef[None], (rows,) + coef.shape), "row")

    outs = interpolate(counts, lists, node_data, centre_data, coefs)
    summed = jnp.sum(exchange(outs, "col").astype(jnp.float32), axis=0)
    ordered = jnp.concatenate([summed[:, :disp_rows], summed[:, 64 : 64 + disp_rows]], axis=0)
    return lax.dot_general(
        ordered.astype(jnp.bfloat16),
        node_pick,
        (((0,), (1,)), ((), ())),
        preferred_element_type=jnp.float32,
    )


def solution(mesh):
    placed = (
        P(None, ("row", "col")),
        P(("row", "col")),
        P("row", "col"),
        P(),
        P(None, ("row", "col")),
    )
    return jax.shard_map(
        per_device, mesh=mesh, in_specs=placed, out_specs=P(None, ("row", "col")), check_vma=False
    )
```

profile of v0, /device:TPU:1, one launch (start us, length us, event | category | flops | bytes accessed | tf_op | source)
XLA Modules:
  0.0 199.7 jit_solution(1490784002359179243)
XLA Ops:
  0.0 0.8 multiply_add_fusion
  0.9 0.8 convert_element_type.109
  2.3 1.2 broadcast_in_dim.170
  3.5 0.8 convert_clamp_fusion
  4.3 0.8 reduce-precision_convert_fusion.1
  5.6 1.7 convert_reduce_fusion.1
  8.8 8.6 %all-to-all-start = ((f32[16,4,256]{2,1,0:T(4,128)}), f32[16,4,256]{2,1,0:T(4,128)S(1)}, u32[]{:S(2)}, u32[]{:S(2)}) async-start(f32[16,4,256]{2,1,0:T(4,128)} %broadcast_in_dim.188), calls=%async_computation | async-start | bytes 131072 | tf_op jit(solution)/shard_map/all_to_all | solution.py:30
  17.9 1.7 convert_reduce_fusion
  19.6 3.0 %fusion.1 = f32[9,2048]{1,0:T(8,128)S(1)} fusion(s32[2048]{0:T(1024)S(1)} %convert_reduce_fusion, bf16[3,2048]{1,0:T(4,128)(2,1)S(1)} %get-tuple-element.58, bf16[3,2048]{1,0:T(4,128)(2,1)S(1)} %get-tuple-element.60, bf16[3,2048]{1,0:T(4,128)(2,1)S(1)} %get-tuple-element.56), kind=kOutput, calls=%fused_computation.3 | convolution fusion | flops 79802368 | bytes 118784 | tf_op jit(solution)/shard_map/dot_general | solution.py:124
  23.9 0.7 broadcast_in_dim.190
  24.6 6.4 %all-to-all-start.1 = ((f32[8,4,2048]{2,1,0:T(4,128)}), f32[8,4,2048]{2,1,0:T(4,128)S(1)}, u32[]{:S(2)}, u32[]{:S(2)}) async-start(f32[8,4,2048]{2,1,0:T(4,128)} %broadcast_in_dim.190), calls=%async_computation.1 | async-start | bytes 524288 | tf_op jit(solution)/shard_map/all_to_all | solution.py:30
  33.4 4.1 %all-to-all-done.1.node_ref = f32[8,4,2048]{2,1,0:T(4,128)S(1)} async-done(((f32[8,4,2048]{2,1,0:T(4,128)}), f32[8,4,2048]{2,1,0:T(4,128)S(1)}, u32[]{:S(2)}, u32[]{:S(2)}) %all-to-all-start.1) | async-done | bytes 262176 | tf_op jit(solution)/shard_map/all_to_all | solution.py:30
  37.5 6.5 %all-to-all-start.2 = ((bf16[128,32,128]{2,1,0:T(8,128)(2,1)}), bf16[128,32,128]{2,1,0:T(8,128)(2,1)S(1)}, u32[]{:S(2)}, u32[]{:S(2)}) async-start(bf16[128,32,128]{2,1,0:T(8,128)(2,1)} %bitcast), calls=%async_computation.2 | async-start | bytes 2097152 | tf_op jit(solution)/shard_map/all_to_all | solution.py:30
  44.2 3.2 %add_reduce_fusion = f32[4,2,4,2048]{3,2,1,0:T(4,128)S(1)} fusion(f32[4,4,2,4,2]{3,4,2,1,0:T(2,128)S(1)} %copy.93, f32[2048]{0:T(1024)S(1)} %bitcast.106, f32[2048]{0:T(1024)S(1)} %bitcast.107, f32[4,4,2,4,2]{3,4,2,1,0:T(2,128)S(1)} %copy.91, f32[4,4,2,4,2]{3,4,2,1,0:T(2,128)S(1)} %copy.89, f32[2048]{0:T(1024)S(1)} %bitcast.108, f32[2048]{0:T(1024)S(1)} %bitcast.109, ...), kind=kLoop, calls=%fused_computation.23 | loop fusion | flops 9371648 | bytes 317440 | tf_op jit(solution)/shard_map/reduce_min | solution.py:152
  48.7 4.1 %select_convert_fusion.1 = (bf16[8,2048,128]{2,1,0:T(8,128)(2,1)S(1)}, bf16[8,2048,128]{2,1,0:T(8,128)(2,1)S(1)}) fusion(s32[2048]{0:T(1024)S(1)} %get-tuple-element.93, s32[8,2048]{1,0:T(8,128)S(1)} %add_select_fusion, s32[2048]{0:T(1024)S(1)} %get-tuple-element.92), kind=kLoop, calls=%fused_computation.13 | loop fusion | flops 10485760 | bytes 8470528 | tf_op jit(solution)/shard_map/convert_element_type | solution.py:173
  52.9 1.6 fusion.3
  54.5 8.8 %all-to-all-done.2 = bf16[128,32,128]{2,1,0:T(8,128)(2,1)S(1)} async-done(((bf16[128,32,128]{2,1,0:T(8,128)(2,1)}), bf16[128,32,128]{2,1,0:T(8,128)(2,1)S(1)}, u32[]{:S(2)}, u32[]{:S(2)}) %all-to-all-start.2) | async-done | bytes 1048608 | tf_op jit(solution)/shard_map/all_to_all | solution.py:30
  65.0 1.7 fusion.126
  66.7 0.7 copy.98
  67.4 0.7 copy.100
  68.2 2.4 %fusion.17 = bf16[8,48,256]{2,1,0:T(8,128)(2,1)S(1)} fusion(bf16[8,512,48]{2,0,1:T(8,128)(2,1)} %get-tuple-element.30, bf16[256]{0:T(256)(128)(2,1)S(1)} %iota_convert_fusion, bf16[8,512]{1,0:T(8,128)(2,1)S(1)} %bitcast.125), kind=kOutput, calls=%fused_computation.26 | convolution fusion | flops 101810176 | bytes 598528 | tf_op jit(solution)/shard_map/dot_general | solution.py:73
  70.5 2.4 %fusion.20 = bf16[8,48,256]{2,1,0:T(8,128)(2,1)S(1)} fusion(bf16[8,512,48]{2,0,1:T(8,128)(2,1)} %get-tuple-element.31, bf16[8,512]{1,0:T(8,128)(2,1)S(1)} %bitcast.124, bf16[256]{0:T(256)(128)(2,1)S(1)} %iota_convert_fusion), kind=kOutput, calls=%fused_computation.27 | convolution fusion | flops 101810176 | bytes 598528 | tf_op jit(solution)/shard_map/dot_general | solution.py:73
  73.0 12.1 %fusion.14 = bf16[48,2048]{1,0:T(8,128)(2,1)S(1)} fusion(s32[2048]{0:T(1024)S(1)} %fusion.73, bf16[48,4096]{1,0:T(8,128)(2,1)S(1)} %bitcast.98, bf16[2048,4096]{1,0:T(8,128)(2,1)} %param.7), kind=kOutput, calls=%fused_computation.21 | convolution fusion | flops 1212350464 | bytes 17375232 | tf_op jit(solution)/shard_map/dot_general | solution.py:326
  85.8 4.3 %all-to-all-start.3 = ((bf16[8,48,256]{2,1,0:T(8,128)(2,1)}), bf16[8,48,256]{2,1,0:T(8,128)(2,1)S(1)}, u32[]{:S(2)}, u32[]{:S(2)}) async-start(bf16[8,48,256]{2,1,0:T(8,128)(2,1)} %bitcast.91), calls=%async_computation.3 | async-start | bytes 393216 | tf_op jit(solution)/shard_map/all_to_all | solution.py:30
  90.1 5.8 %all-to-all-done.3 = bf16[8,48,256]{2,1,0:T(8,128)(2,1)S(1)} async-done(((bf16[8,48,256]{2,1,0:T(8,128)(2,1)}), bf16[8,48,256]{2,1,0:T(8,128)(2,1)S(1)}, u32[]{:S(2)}, u32[]{:S(2)}) %all-to-all-start.3) | async-done | bytes 196640 | tf_op jit(solution)/shard_map/all_to_all | solution.py:30
  96.0 0.8 broadcast_in_dim.199
  96.8 3.6 %all-to-all-start.4 = ((bf16[16,48,256]{2,1,0:T(8,128)(2,1)}), bf16[16,48,256]{2,1,0:T(8,128)(2,1)S(1)}, u32[]{:S(2)}, u32[]{:S(2)}) async-start(bf16[16,48,256]{2,1,0:T(8,128)(2,1)} %broadcast_in_dim.199), calls=%async_computation.4 | async-start | bytes 786432 | tf_op jit(solution)/shard_map/all_to_all | solution.py:30
  101.0 8.5 %all-to-all-done.4.coef_ref = bf16[16,48,256]{2,1,0:T(8,128)(2,1)S(1)} async-done(((bf16[16,48,256]{2,1,0:T(8,128)(2,1)}), bf16[16,48,256]{2,1,0:T(8,128)(2,1)S(1)}, u32[]{:S(2)}, u32[]{:S(2)}) %all-to-all-start.4) | async-done | bytes 393248 | tf_op jit(solution)/shard_map/all_to_all | solution.py:30
  109.5 0.7 copy-done.1
  110.3 50.4 %interpolate.1 = bf16[8,1024,128]{2,1,0:T(8,128)(2,1)} custom-call(s32[8]{0:T(128)} %bitcast.129, s32[8,2080]{1,0:T(8,128)} %pad_select_fusion.list_ref, f32[8,4,2048]{2,1,0:T(4,128)} %copy-done.2, f32[16,4,256]{2,1,0:T(4,128)} %copy-done.3, bf16[16,48,256]{2,1,0:T(8,128)(2,1)} %copy-done.1), custom_call_target="tpu_custom_call" | custom-call | tf_op jit(solution)/shard_map/interpolate/pallas_call | solution.py:276
  160.7 34.0 %all_to_all.30 = bf16[8,1024,128]{2,1,0:T(8,128)(2,1)S(1)} all-to-all(bf16[8,1024,128]{2,1,0:T(8,128)(2,1)} %interpolate.1), channel_id=1, replica_groups=mesh['row'=16,'col'=8] {'col'}, dimensions={0} | all-to-all | bytes 4194304 | tf_op jit(solution)/shard_map/all_to_all | solution.py:30
  195.4 4.2 %fusion = f32[48,2048]{1,0:T(8,128)} fusion(s32[2048]{0:T(1024)S(1)} %convert_reduce_fusion, bf16[1024,48]{0,1:T(8,128)(2,1)S(1)} %copy.104, bf16[1024,48]{0,1:T(8,128)(2,1)S(1)} %copy.103), kind=kOutput, calls=%fused_computation.2 | convolution fusion | flops 407240704 | bytes 598016 | tf_op jit(solution)/shard_map/dot_general | solution.py:335
  (115 shorter events, 11.9 us)
Async XLA Ops:
  0.0 2.2 %copy-start = (f32[3,32768]{1,0:T(4,128)S(1)}, f32[3,32768]{1,0:T(4,128)}, u32[]{:S(2)}) copy-start(f32[3,32768]{1,0:T(4,128)} %param.8) | copy-start | bytes 1179652
  8.8 15.1 %all-to-all-start = ((f32[16,4,256]{2,1,0:T(4,128)}), f32[16,4,256]{2,1,0:T(4,128)S(1)}, u32[]{:S(2)}, u32[]{:S(2)}) async-start(f32[16,4,256]{2,1,0:T(4,128)} %broadcast_in_dim.188), calls=%async_computation | async-start | bytes 131072 | tf_op jit(solution)/shard_map/all_to_all | solution.py:30
  23.9 29.0 %copy-start.3 = (f32[16,4,256]{2,1,0:T(4,128)}, f32[16,4,256]{2,1,0:T(4,128)S(1)}, u32[]{:S(2)}) copy-start(f32[16,4,256]{2,1,0:T(4,128)S(1)} %all-to-all-done.centre_ref) | copy-start | bytes 196612
  24.6 12.9 %all-to-all-start.1 = ((f32[8,4,2048]{2,1,0:T(4,128)}), f32[8,4,2048]{2,1,0:T(4,128)S(1)}, u32[]{:S(2)}, u32[]{:S(2)}) async-start(f32[8,4,2048]{2,1,0:T(4,128)} %broadcast_in_dim.190), calls=%async_computation.1 | async-start | bytes 524288 | tf_op jit(solution)/shard_map/all_to_all | solution.py:30
  37.5 15.4 %copy-start.2 = (f32[8,4,2048]{2,1,0:T(4,128)}, f32[8,4,2048]{2,1,0:T(4,128)S(1)}, u32[]{:S(2)}) copy-start(f32[8,4,2048]{2,1,0:T(4,128)S(1)} %all-to-all-done.1.node_ref) | copy-start | bytes 786436
  37.5 25.8 %all-to-all-start.2 = ((bf16[128,32,128]{2,1,0:T(8,128)(2,1)}), bf16[128,32,128]{2,1,0:T(8,128)(2,1)S(1)}, u32[]{:S(2)}, u32[]{:S(2)}) async-start(bf16[128,32,128]{2,1,0:T(8,128)(2,1)} %bitcast), calls=%async_computation.2 | async-start | bytes 2097152 | tf_op jit(solution)/shard_map/all_to_all | solution.py:30
  48.7 51.6 %copy-start.4 = (s32[8,1]{0,1:T(1,128)}, s32[8,1]{0,1:T(1,128)S(1)}, u32[]{:S(2)}) copy-start(s32[8,1]{0,1:T(1,128)S(1)} %copy.119) | copy-start | bytes 100
  85.8 10.1 %all-to-all-start.3 = ((bf16[8,48,256]{2,1,0:T(8,128)(2,1)}), bf16[8,48,256]{2,1,0:T(8,128)(2,1)S(1)}, u32[]{:S(2)}, u32[]{:S(2)}) async-start(bf16[8,48,256]{2,1,0:T(8,128)(2,1)} %bitcast.91), calls=%async_computation.3 | async-start | bytes 393216 | tf_op jit(solution)/shard_map/all_to_all | solution.py:30
  96.8 12.8 %all-to-all-start.4 = ((bf16[16,48,256]{2,1,0:T(8,128)(2,1)}), bf16[16,48,256]{2,1,0:T(8,128)(2,1)S(1)}, u32[]{:S(2)}, u32[]{:S(2)}) async-start(bf16[16,48,256]{2,1,0:T(8,128)(2,1)} %broadcast_in_dim.199), calls=%async_computation.4 | async-start | bytes 786432 | tf_op jit(solution)/shard_map/all_to_all | solution.py:30
  109.5 0.7 copy-start.1
where the time goes:
time: 202 us; the launch traced here: 200 us
  Pallas kernels  50.4 us (25%)
  blocking collectives  34 us (17%)
  starting transfers between devices  29.3 us (15%)
  waiting for transfers between devices  27.9 us (14%)
  matrix products  26.6 us (13%)
  other arithmetic  17.1 us (8%)
  local copies, waits for them, and re-layouts  13.8 us (7%)
    pallas_call x1, Pallas kernels, interpolate(): pl.pallas_call(kernel, out_shape=jax.ShapeDtypeStruct((cols, nodes // 2,...  50.4 us
    all_to_all x1, blocking collectives, exchange(): return lax.all_to_all(value, axes, split_axis=0, concat_axis=0, tiled=True)  34 us
    all_to_all x5, starting transfers between devices, exchange(): return lax.all_to_all(value, axes, split_axis=0, concat_axis=0, tiled=True)  29.3 us
    all_to_all x5, waiting for transfers between devices, exchange(): return lax.all_to_all(value, axes, split_axis=0, concat_axis=0, tiled=True)  27.9 us
    dot_general x1, matrix products, per_device(): jnp.dot(partial.astype(jnp.bfloat16), centre_pick, preferred_element_type...  12.1 us
    dot_general x2, matrix products, column_displacements(): lax.dot_general(part[:, :, :disp_rows], place, (((1,), (1,)), ((0,), (0,)...  4.71 us
    dot_general x1, matrix products, per_device(): lax.dot_general(ordered.astype(jnp.bfloat16), node_pick, (((0,), (1,)), (...  4.24 us
    convert_element_type x1, other arithmetic, near_groups(): jnp.where(minor, d[None, :, None], 0).astype(jnp.bfloat16)  4.13 us
  transfers between devices with their start and end apart: 5, of which 5 were waited for; matrix products, arithmetic and copies ran while one was open for 10% of the time, Pallas kernels for 0%

commit v1 on v0

--- a/solution.py
+++ b/solution.py
@@ -6,6 +6,7 @@
 from jax.experimental import pallas as pl
 from jax.experimental.pallas import tpu as pltpu
 from jax.sharding import PartitionSpec as P
+
 
 M = 32768
 CAP = 4
@@ -325,7 +326,8 @@
     )
     partial = jnp.dot(partial.astype(jnp.bfloat16), centre_pick, preferred_element_type=jnp.float32)
     partial = partial.astype(jnp.bfloat16).reshape(disp_rows, cols, piece).transpose(1, 0, 2)
-    coef = jnp.sum(exchange(partial, "col").astype(jnp.float32), axis=0)
+    partial = exchange(partial, "col")
+    coef = jnp.sum(partial.astype(jnp.float32), axis=0)
     coef = lax.optimization_barrier(coef).astype(jnp.bfloat16)
     coefs = exchange(jnp.broadcast_to(coef[None], (rows,) + coef.shape), "row")
 
@@ -348,6 +350,4 @@
         P(),
         P(None, ("row", "col")),
     )
-    return jax.shard_map(
-        per_device, mesh=mesh, in_specs=placed, out_specs=P(None, ("row", "col")), check_vma=False
-    )
+    return jax.shard_map(per_device, mesh=mesh, in_specs=placed, out_specs=P(None, ("row", "col")), check_vma=False)

time: 202 us -> 198 us (0.980)
  blocking collectives: 34 us -> 28 us
  Pallas kernels: 50.4 us -> 53.4 us
    all_to_all x1, blocking collectives: 34 us -> 28 us  [exchange(): return lax.all_to_all(value, axes, split_axis=0, concat_axis=0, tiled=True)]
    pallas_call x1, Pallas kernels: 50.4 us -> 53.4 us  [interpolate(): pl.pallas_call(kernel, out_shape=jax.ShapeDtypeStruct((cols, nodes // 2,...]
where the time goes in v1:
time: 198 us; the launch traced here: 197 us
  Pallas kernels  53.4 us (27%)
  starting transfers between devices  29.3 us (15%)
  blocking collectives  28 us (14%)
  waiting for transfers between devices  27.9 us (14%)
  matrix products  26.6 us (13%)
  other arithmetic  17.1 us (9%)
  local copies, waits for them, and re-layouts  13.8 us (7%)
    pallas_call x1, Pallas kernels, interpolate(): pl.pallas_call(kernel, out_shape=jax.ShapeDtypeStruct((cols, nodes // 2,...  53.4 us
    all_to_all x5, starting transfers between devices, exchange(): return lax.all_to_all(value, axes, split_axis=0, concat_axis=0, tiled=True)  29.3 us
    all_to_all x1, blocking collectives, exchange(): return lax.all_to_all(value, axes, split_axis=0, concat_axis=0, tiled=True)  28 us
    all_to_all x5, waiting for transfers between devices, exchange(): return lax.all_to_all(value, axes, split_axis=0, concat_axis=0, tiled=True)  27.9 us
    dot_general x1, matrix products, per_device(): jnp.dot(partial.astype(jnp.bfloat16), centre_pick, preferred_element_type...  12.1 us
    dot_general x2, matrix products, column_displacements(): lax.dot_general(part[:, :, :disp_rows], place, (((1,), (1,)), ((0,), (0,)...  4.71 us
    dot_general x1, matrix products, per_device(): lax.dot_general(ordered.astype(jnp.bfloat16), node_pick, (((0,), (1,)), (...  4.24 us
    convert_element_type x1, other arithmetic, near_groups(): jnp.where(minor, d[None, :, None], 0).astype(jnp.bfloat16)  4.13 us
  transfers between devices with their start and end apart: 5, of which 5 were waited for; matrix products, arithmetic and copies ran while one was open for 10% of the time, Pallas kernels for 0%

profile of v1, /device:TPU:1, one launch (start us, length us, event | category | flops | bytes accessed | tf_op | source)
XLA Modules:
  0.0 196.7 jit_solution(1490784002359179243)
XLA Ops:
  0.0 0.8 multiply_add_fusion
  0.9 0.8 convert_element_type.109
  2.3 1.2 broadcast_in_dim.170
  3.5 0.8 convert_clamp_fusion
  4.3 0.8 reduce-precision_convert_fusion.1
  5.6 1.7 convert_reduce_fusion.1
  8.8 8.6 %all-to-all-start = ((f32[16,4,256]{2,1,0:T(4,128)}), f32[16,4,256]{2,1,0:T(4,128)S(1)}, u32[]{:S(2)}, u32[]{:S(2)}) async-start(f32[16,4,256]{2,1,0:T(4,128)} %broadcast_in_dim.188), calls=%async_computation | async-start | bytes 131072 | tf_op jit(solution)/shard_map/all_to_all | solution.py:31
  17.9 1.7 convert_reduce_fusion
  19.6 3.0 %fusion.1 = f32[9,2048]{1,0:T(8,128)S(1)} fusion(s32[2048]{0:T(1024)S(1)} %convert_reduce_fusion, bf16[3,2048]{1,0:T(4,128)(2,1)S(1)} %get-tuple-element.58, bf16[3,2048]{1,0:T(4,128)(2,1)S(1)} %get-tuple-element.60, bf16[3,2048]{1,0:T(4,128)(2,1)S(1)} %get-tuple-element.56), kind=kOutput, calls=%fused_computation.3 | convolution fusion | flops 79802368 | bytes 118784 | tf_op jit(solution)/shard_map/dot_general | solution.py:125
  23.9 0.7 broadcast_in_dim.190
  24.6 6.4 %all-to-all-start.1 = ((f32[8,4,2048]{2,1,0:T(4,128)}), f32[8,4,2048]{2,1,0:T(4,128)S(1)}, u32[]{:S(2)}, u32[]{:S(2)}) async-start(f32[8,4,2048]{2,1,0:T(4,128)} %broadcast_in_dim.190), calls=%async_computation.1 | async-start | bytes 524288 | tf_op jit(solution)/shard_map/all_to_all | solution.py:31
  33.4 4.1 %all-to-all-done.1.node_ref = f32[8,4,2048]{2,1,0:T(4,128)S(1)} async-done(((f32[8,4,2048]{2,1,0:T(4,128)}), f32[8,4,2048]{2,1,0:T(4,128)S(1)}, u32[]{:S(2)}, u32[]{:S(2)}) %all-to-all-start.1) | async-done | bytes 262176 | tf_op jit(solution)/shard_map/all_to_all | solution.py:31
  37.5 6.5 %all-to-all-start.2 = ((bf16[128,32,128]{2,1,0:T(8,128)(2,1)}), bf16[128,32,128]{2,1,0:T(8,128)(2,1)S(1)}, u32[]{:S(2)}, u32[]{:S(2)}) async-start(bf16[128,32,128]{2,1,0:T(8,128)(2,1)} %bitcast), calls=%async_computation.2 | async-start | bytes 2097152 | tf_op jit(solution)/shard_map/all_to_all | solution.py:31
  44.2 3.2 %add_reduce_fusion = f32[4,2,4,2048]{3,2,1,0:T(4,128)S(1)} fusion(f32[4,4,2,4,2]{3,4,2,1,0:T(2,128)S(1)} %copy.93, f32[2048]{0:T(1024)S(1)} %bitcast.106, f32[2048]{0:T(1024)S(1)} %bitcast.107, f32[4,4,2,4,2]{3,4,2,1,0:T(2,128)S(1)} %copy.91, f32[4,4,2,4,2]{3,4,2,1,0:T(2,128)S(1)} %copy.89, f32[2048]{0:T(1024)S(1)} %bitcast.108, f32[2048]{0:T(1024)S(1)} %bitcast.109, ...), kind=kLoop, calls=%fused_computation.23 | loop fusion | flops 9371648 | bytes 317440 | tf_op jit(solution)/shard_map/reduce_min | solution.py:153
  48.7 4.1 %select_convert_fusion.1 = (bf16[8,2048,128]{2,1,0:T(8,128)(2,1)S(1)}, bf16[8,2048,128]{2,1,0:T(8,128)(2,1)S(1)}) fusion(s32[2048]{0:T(1024)S(1)} %get-tuple-element.93, s32[8,2048]{1,0:T(8,128)S(1)} %add_select_fusion, s32[2048]{0:T(1024)S(1)} %get-tuple-element.92), kind=kLoop, calls=%fused_computation.13 | loop fusion | flops 10485760 | bytes 8470528 | tf_op jit(solution)/shard_map/convert_element_type | solution.py:174
  52.9 1.6 fusion.3
  54.5 8.8 %all-to-all-done.2 = bf16[128,32,128]{2,1,0:T(8,128)(2,1)S(1)} async-done(((bf16[128,32,128]{2,1,0:T(8,128)(2,1)}), bf16[128,32,128]{2,1,0:T(8,128)(2,1)S(1)}, u32[]{:S(2)}, u32[]{:S(2)}) %all-to-all-start.2) | async-done | bytes 1048608 | tf_op jit(solution)/shard_map/all_to_all | solution.py:31
  65.0 1.7 fusion.126
  66.7 0.7 copy.98
  67.4 0.7 copy.100
  68.2 2.4 %fusion.17 = bf16[8,48,256]{2,1,0:T(8,128)(2,1)S(1)} fusion(bf16[8,512,48]{2,0,1:T(8,128)(2,1)} %get-tuple-element.30, bf16[256]{0:T(256)(128)(2,1)S(1)} %iota_convert_fusion, bf16[8,512]{1,0:T(8,128)(2,1)S(1)} %bitcast.125), kind=kOutput, calls=%fused_computation.26 | convolution fusion | flops 101810176 | bytes 598528 | tf_op jit(solution)/shard_map/dot_general | solution.py:74
  70.5 2.4 %fusion.20 = bf16[8,48,256]{2,1,0:T(8,128)(2,1)S(1)} fusion(bf16[8,512,48]{2,0,1:T(8,128)(2,1)} %get-tuple-element.31, bf16[8,512]{1,0:T(8,128)(2,1)S(1)} %bitcast.124, bf16[256]{0:T(256)(128)(2,1)S(1)} %iota_convert_fusion), kind=kOutput, calls=%fused_computation.27 | convolution fusion | flops 101810176 | bytes 598528 | tf_op jit(solution)/shard_map/dot_general | solution.py:74
  73.0 12.1 %fusion.14 = bf16[48,2048]{1,0:T(8,128)(2,1)S(1)} fusion(s32[2048]{0:T(1024)S(1)} %fusion.73, bf16[48,4096]{1,0:T(8,128)(2,1)S(1)} %bitcast.98, bf16[2048,4096]{1,0:T(8,128)(2,1)} %param.7), kind=kOutput, calls=%fused_computation.21 | convolution fusion | flops 1212350464 | bytes 17375232 | tf_op jit(solution)/shard_map/dot_general | solution.py:327
  85.8 4.3 %all-to-all-start.3 = ((bf16[8,48,256]{2,1,0:T(8,128)(2,1)}), bf16[8,48,256]{2,1,0:T(8,128)(2,1)S(1)}, u32[]{:S(2)}, u32[]{:S(2)}) async-start(bf16[8,48,256]{2,1,0:T(8,128)(2,1)} %bitcast.91), calls=%async_computation.3 | async-start | bytes 393216 | tf_op jit(solution)/shard_map/all_to_all | solution.py:31
  90.1 5.8 %all-to-all-done.3 = bf16[8,48,256]{2,1,0:T(8,128)(2,1)S(1)} async-done(((bf16[8,48,256]{2,1,0:T(8,128)(2,1)}), bf16[8,48,256]{2,1,0:T(8,128)(2,1)S(1)}, u32[]{:S(2)}, u32[]{:S(2)}) %all-to-all-start.3) | async-done | bytes 196640 | tf_op jit(solution)/shard_map/all_to_all | solution.py:31
  96.0 0.8 broadcast_in_dim.199
  96.8 3.6 %all-to-all-start.4 = ((bf16[16,48,256]{2,1,0:T(8,128)(2,1)}), bf16[16,48,256]{2,1,0:T(8,128)(2,1)S(1)}, u32[]{:S(2)}, u32[]{:S(2)}) async-start(bf16[16,48,256]{2,1,0:T(8,128)(2,1)} %broadcast_in_dim.199), calls=%async_computation.4 | async-start | bytes 786432 | tf_op jit(solution)/shard_map/all_to_all | solution.py:31
  101.0 8.5 %all-to-all-done.4.coef_ref = bf16[16,48,256]{2,1,0:T(8,128)(2,1)S(1)} async-done(((bf16[16,48,256]{2,1,0:T(8,128)(2,1)}), bf16[16,48,256]{2,1,0:T(8,128)(2,1)S(1)}, u32[]{:S(2)}, u32[]{:S(2)}) %all-to-all-start.4) | async-done | bytes 393248 | tf_op jit(solution)/shard_map/all_to_all | solution.py:31
  109.5 0.7 copy-done.1
  110.3 53.4 %interpolate.1 = bf16[8,1024,128]{2,1,0:T(8,128)(2,1)} custom-call(s32[8]{0:T(128)} %bitcast.129, s32[8,2080]{1,0:T(8,128)} %pad_select_fusion.list_ref, f32[8,4,2048]{2,1,0:T(4,128)} %copy-done.2, f32[16,4,256]{2,1,0:T(4,128)} %copy-done.3, bf16[16,48,256]{2,1,0:T(8,128)(2,1)} %copy-done.1), custom_call_target="tpu_custom_call" | custom-call | tf_op jit(solution)/shard_map/interpolate/pallas_call | solution.py:277
  163.7 28.0 %all_to_all.30 = bf16[8,1024,128]{2,1,0:T(8,128)(2,1)S(1)} all-to-all(bf16[8,1024,128]{2,1,0:T(8,128)(2,1)} %interpolate.1), channel_id=1, replica_groups=mesh['row'=16,'col'=8] {'col'}, dimensions={0} | all-to-all | bytes 4194304 | tf_op jit(solution)/shard_map/all_to_all | solution.py:31
  192.4 4.2 %fusion = f32[48,2048]{1,0:T(8,128)} fusion(s32[2048]{0:T(1024)S(1)} %convert_reduce_fusion, bf16[1024,48]{0,1:T(8,128)(2,1)S(1)} %copy.104, bf16[1024,48]{0,1:T(8,128)(2,1)S(1)} %copy.103), kind=kOutput, calls=%fused_computation.2 | convolution fusion | flops 407240704 | bytes 598016 | tf_op jit(solution)/shard_map/dot_general | solution.py:337
  (115 shorter events, 11.9 us)
Async XLA Ops:
  0.0 2.2 %copy-start = (f32[3,32768]{1,0:T(4,128)S(1)}, f32[3,32768]{1,0:T(4,128)}, u32[]{:S(2)}) copy-start(f32[3,32768]{1,0:T(4,128)} %param.8) | copy-start | bytes 1179652
  8.8 15.1 %all-to-all-start = ((f32[16,4,256]{2,1,0:T(4,128)}), f32[16,4,256]{2,1,0:T(4,128)S(1)}, u32[]{:S(2)}, u32[]{:S(2)}) async-start(f32[16,4,256]{2,1,0:T(4,128)} %broadcast_in_dim.188), calls=%async_computation | async-start | bytes 131072 | tf_op jit(solution)/shard_map/all_to_all | solution.py:31
  23.9 29.0 %copy-start.3 = (f32[16,4,256]{2,1,0:T(4,128)}, f32[16,4,256]{2,1,0:T(4,128)S(1)}, u32[]{:S(2)}) copy-start(f32[16,4,256]{2,1,0:T(4,128)S(1)} %all-to-all-done.centre_ref) | copy-start | bytes 196612
  24.6 12.9 %all-to-all-start.1 = ((f32[8,4,2048]{2,1,0:T(4,128)}), f32[8,4,2048]{2,1,0:T(4,128)S(1)}, u32[]{:S(2)}, u32[]{:S(2)}) async-start(f32[8,4,2048]{2,1,0:T(4,128)} %broadcast_in_dim.190), calls=%async_computation.1 | async-start | bytes 524288 | tf_op jit(solution)/shard_map/all_to_all | solution.py:31
  37.5 15.4 %copy-start.2 = (f32[8,4,2048]{2,1,0:T(4,128)}, f32[8,4,2048]{2,1,0:T(4,128)S(1)}, u32[]{:S(2)}) copy-start(f32[8,4,2048]{2,1,0:T(4,128)S(1)} %all-to-all-done.1.node_ref) | copy-start | bytes 786436
  37.5 25.8 %all-to-all-start.2 = ((bf16[128,32,128]{2,1,0:T(8,128)(2,1)}), bf16[128,32,128]{2,1,0:T(8,128)(2,1)S(1)}, u32[]{:S(2)}, u32[]{:S(2)}) async-start(bf16[128,32,128]{2,1,0:T(8,128)(2,1)} %bitcast), calls=%async_computation.2 | async-start | bytes 2097152 | tf_op jit(solution)/shard_map/all_to_all | solution.py:31
  48.7 51.6 %copy-start.4 = (s32[8,1]{0,1:T(1,128)}, s32[8,1]{0,1:T(1,128)S(1)}, u32[]{:S(2)}) copy-start(s32[8,1]{0,1:T(1,128)S(1)} %copy.119) | copy-start | bytes 100
  85.8 10.1 %all-to-all-start.3 = ((bf16[8,48,256]{2,1,0:T(8,128)(2,1)}), bf16[8,48,256]{2,1,0:T(8,128)(2,1)S(1)}, u32[]{:S(2)}, u32[]{:S(2)}) async-start(bf16[8,48,256]{2,1,0:T(8,128)(2,1)} %bitcast.91), calls=%async_computation.3 | async-start | bytes 393216 | tf_op jit(solution)/shard_map/all_to_all | solution.py:31
  96.8 12.8 %all-to-all-start.4 = ((bf16[16,48,256]{2,1,0:T(8,128)(2,1)}), bf16[16,48,256]{2,1,0:T(8,128)(2,1)S(1)}, u32[]{:S(2)}, u32[]{:S(2)}) async-start(bf16[16,48,256]{2,1,0:T(8,128)(2,1)} %broadcast_in_dim.199), calls=%async_computation.4 | async-start | bytes 786432 | tf_op jit(solution)/shard_map/all_to_all | solution.py:31
  109.5 0.7 copy-start.1

commit v2 on v1

--- a/solution.py
+++ b/solution.py
@@ -153,7 +153,11 @@
     apart = jnp.min(apart, axis=(0, 4))
     turned = [jnp.roll(apart[k], -k, axis=1) for k in range(turns)]
     apart = jnp.minimum(jnp.minimum(turned[0], turned[1]), jnp.minimum(turned[2], turned[3]))
-    near = apart.reshape(piece // BLOCK, total) <= RADIUS * RADIUS * 1.001
+    return apart.reshape(piece // BLOCK, total) <= RADIUS * RADIUS * 1.001
+
+
+def listed_groups(near):
+    total = near.shape[1]
     blocks = near.shape[0]
     spans = total // LANES
     ones = near.astype(jnp.bfloat16).reshape(blocks * spans, LANES)
@@ -184,14 +188,35 @@
     return counts, jnp.where(slots[None, :] < counts[:, None], listed, total)
 
 
-def interpolate(counts, lists, node_data, centre_data, coefs):
+def interpolate(parity, counts, lists, node_data, centre_data, coefs):
     rows, disp_rows, piece = coefs.shape
     cols, _, nodes = node_data.shape
     total = cols * nodes
+    last = total // GROUP
     turns = LANES // BLOCK
     quads = rows // turns
-
-    def kernel(count_ref, list_ref, node_ref, centre_ref, coef_ref, out_ref, acc_ref, row_ref, place_ref, weight_ref):
+    blocks = piece // BLOCK
+    size = GROUP * BATCH
+
+    def kernel(
+        parity_ref,
+        count_ref,
+        list_ref,
+        node_ref,
+        centre_ref,
+        coef_ref,
+        own_ref,
+        other_ref,
+        acc_ref,
+        row_ref,
+        place_ref,
+        weight_ref,
+        phi_0,
+        phi_1,
+        spread_0,
+        spread_1,
+        table_ref,
+    ):
         acc_ref[total:, :] = jnp.zeros((GROUP, LANES), jnp.float32)
         for col in range(cols):
 
@@ -214,79 +239,126 @@
                 value = jnp.where(segment == k, take((k - block) % turns), value)
             return value
 
-        for block in range(piece // BLOCK):
+        def fill(number, block, start):
+            table_ref[0, number] = block
+            table_ref[1, number] = start
+
+        fill(0, 0, last)
+        number = 1
+        for block in range(blocks):
             lanes = slice(block // turns * LANES, (block // turns + 1) * LANES)
             for quad in range(quads):
                 coef = gather(lambda k: coef_ref[turns * quad + k, :, lanes].astype(jnp.float32), block)
-                weight_ref[:, quad * LANES : (quad + 1) * LANES] = coef.astype(jnp.bfloat16)
+                weight_ref[block, :, quad * LANES : (quad + 1) * LANES] = coef.astype(jnp.bfloat16)
                 for axis in range(3):
                     centre = gather(lambda k: centre_ref[turns * quad + k, axis : axis + 1, lanes], block)
-                    place_ref[3 * quad + axis : 3 * quad + axis + 1, :] = centre * SCALE
-
-            def batch(step, carry):
-                ids = [list_ref[block, step * BATCH + i] for i in range(BATCH)]
-                node = jnp.concatenate(
-                    [
-                        row_ref[pl.ds(pl.multiple_of(jnp.minimum(i, total // GROUP - 1) * GROUP, GROUP), GROUP), :]
-                        for i in ids
-                    ],
-                    axis=0,
+                    row = 16 * block + 3 * quad + axis
+                    place_ref[row : row + 1, :] = centre * SCALE
+
+            def add(step, place):
+                fill(place, block, step * BATCH)
+                return place + 1
+
+            number = lax.fori_loop(0, (count_ref[block] + BATCH - 1) // BATCH, add, number)
+        for extra in range(3):
+            fill(number + extra, 0, last)
+
+        def ids(place):
+            block = table_ref[0, place]
+            start = table_ref[1, place]
+            return [list_ref[block, start + i] for i in range(BATCH)]
+
+        def spread(place, spread_ref):
+            node = jnp.concatenate(
+                [
+                    row_ref[pl.ds(pl.multiple_of(jnp.minimum(i, last - 1) * GROUP, GROUP), GROUP), :]
+                    for i in ids(place)
+                ],
+                axis=0,
+            )
+            for axis in range(3):
+                spread_ref[axis * size : (axis + 1) * size, :] = jnp.broadcast_to(
+                    node[:, axis : axis + 1], (size, LANES)
                 )
-                node = [jnp.broadcast_to(node[:, a : a + 1], (GROUP * BATCH, LANES)) for a in range(3)]
-                part = jnp.zeros((GROUP * BATCH, disp_rows), jnp.float32)
-                for pair in range(quads // 2):
-                    tiles = []
-                    for quad in (2 * pair, 2 * pair + 1):
-                        squared = None
-                        for axis in range(3):
-                            difference = node[axis] - place_ref[3 * quad + axis : 3 * quad + axis + 1, :]
-                            square = difference * difference
-                            squared = square if squared is None else squared + square
-                        scaled = squared * lax.rsqrt(jnp.maximum(squared, 1e-30))
-                        remain = jnp.maximum(4.0 - scaled, 0.0)
-                        remain = remain * remain
-                        tiles.append((remain * remain * (scaled + 1.0)).astype(jnp.bfloat16))
-                    part = part + lax.dot_general(
-                        jnp.concatenate(tiles, axis=1),
-                        weight_ref[:, pair * 2 * LANES : (pair + 1) * 2 * LANES],
-                        (((1,), (1,)), ((), ())),
-                        preferred_element_type=jnp.float32,
-                    )
-                for i, number in enumerate(ids):
-                    start = pl.multiple_of(number * GROUP, GROUP)
-                    acc_ref[pl.ds(start, GROUP), :disp_rows] += part[i * GROUP : (i + 1) * GROUP]
-                return carry
-
-            lax.fori_loop(0, (count_ref[block] + BATCH - 1) // BATCH, batch, 0)
+
+        def evaluate(place, spread_ref, phi_ref):
+            block = table_ref[0, place]
+            for quad in range(quads):
+                squared = None
+                for axis in range(3):
+                    centre = place_ref[pl.ds(16 * block + 3 * quad + axis, 1), :]
+                    difference = spread_ref[axis * size : (axis + 1) * size, :] - centre
+                    square = difference * difference
+                    squared = square if squared is None else squared + square
+                scaled = squared * lax.rsqrt(jnp.maximum(squared, 1e-30))
+                remain = jnp.maximum(4.0 - scaled, 0.0)
+                remain = remain * remain
+                phi = remain * remain * (scaled + 1.0)
+                phi_ref[:, quad * LANES : (quad + 1) * LANES] = phi.astype(jnp.bfloat16)
+
+        def collect(place, phi_ref):
+            block = table_ref[0, place]
+            part = lax.dot_general(
+                phi_ref[...],
+                weight_ref[block],
+                (((1,), (1,)), ((), ())),
+                preferred_element_type=jnp.float32,
+            )
+            for i, group in enumerate(ids(place)):
+                start = pl.multiple_of(group * GROUP, GROUP)
+                acc_ref[pl.ds(start, GROUP), :disp_rows] += part[i * GROUP : (i + 1) * GROUP]
+
+        spread(1, spread_0)
+
+        def two(step, carry):
+            place = 2 * step + 1
+            collect(place - 1, phi_1)
+            evaluate(place, spread_0, phi_0)
+            spread(place + 1, spread_1)
+            collect(place, phi_0)
+            evaluate(place + 1, spread_1, phi_1)
+            spread(place + 2, spread_0)
+            return carry
+
+        lax.fori_loop(0, (number + 1) // 2, two, 0)
 
         low_lanes = lane < LANES // 2
-        for col in range(cols):
-
-            def pack(step, carry):
-                first = pl.multiple_of(step * LANES, LANES)
-                low = acc_ref[pl.ds(col * nodes + first, LANES), :]
-                high = acc_ref[pl.ds(col * nodes + nodes // 2 + first, LANES), :]
-                both = jnp.where(low_lanes, low, pltpu.roll(high, LANES // 2, 1))
-                out_ref[col, pl.ds(first, LANES), :] = (both * (1.0 / 256.0)).astype(jnp.bfloat16)
-                return carry
-
-            lax.fori_loop(0, nodes // 2 // LANES, pack, 0)
+        for side, out_ref in enumerate((own_ref, other_ref)):
+            for chip in range(cols // 2):
+                col = 2 * chip + (parity_ref[0] + side) % 2
+
+                def pack(step, carry):
+                    first = pl.multiple_of(step * LANES, LANES)
+                    start = pl.multiple_of(col * nodes, nodes) + first
+                    low = acc_ref[pl.ds(start, LANES), :]
+                    high = acc_ref[pl.ds(start + nodes // 2, LANES), :]
+                    both = jnp.where(low_lanes, low, pltpu.roll(high, LANES // 2, 1))
+                    out_ref[chip, pl.ds(first, LANES), :] = (both * (1.0 / 256.0)).astype(jnp.bfloat16)
+                    return carry
+
+                lax.fori_loop(0, nodes // 2 // LANES, pack, 0)
 
     vmem = pl.BlockSpec(memory_space=pltpu.VMEM)
     smem = pl.BlockSpec(memory_space=pltpu.SMEM)
+    out = jax.ShapeDtypeStruct((cols // 2, nodes // 2, LANES), jnp.bfloat16)
     return pl.pallas_call(
         kernel,
-        out_shape=jax.ShapeDtypeStruct((cols, nodes // 2, LANES), jnp.bfloat16),
-        in_specs=[smem, smem, vmem, vmem, vmem],
-        out_specs=vmem,
+        out_shape=(out, out),
+        in_specs=[smem, smem, smem, vmem, vmem, vmem],
+        out_specs=(vmem, vmem),
         scratch_shapes=[
             pltpu.VMEM((total + GROUP, LANES), jnp.float32),
             pltpu.VMEM((total, 8), jnp.float32),
-            pltpu.VMEM((16, LANES), jnp.float32),
-            pltpu.VMEM((disp_rows, quads * LANES), jnp.bfloat16),
+            pltpu.VMEM((16 * blocks, LANES), jnp.float32),
+            pltpu.VMEM((blocks, disp_rows, quads * LANES), jnp.bfloat16),
+            pltpu.VMEM((size, quads * LANES), jnp.bfloat16),
+            pltpu.VMEM((size, quads * LANES), jnp.bfloat16),
+            pltpu.VMEM((3 * size, LANES), jnp.float32),
+            pltpu.VMEM((3 * size, LANES), jnp.float32),
+            pltpu.SMEM((2, blocks * (last // BATCH) + 4), jnp.int32),
         ],
         name="interpolate",
-    )(counts, lists, node_data, centre_data, coefs)
+    )(parity, counts, lists, node_data, centre_data, coefs)
 
 
 def per_device(struct_disp, target, inverse, centre_xyz, node_xyz):
@@ -318,7 +390,8 @@
     node_pick = (node_rank[:, None] == node_order[None, :]).astype(jnp.bfloat16)
     own_nodes = with_boxes(pick_columns(node_xyz, node_pick), GROUP)
     node_data = exchange(jnp.broadcast_to(own_nodes[None], (cols, 4, nodes)), "col")
-    counts, lists = near_groups(centre_data, node_data)
+    near = near_groups(centre_data, node_data)
+    counts, lists = listed_groups(near)
 
     disp_bf = column_displacements(recv, disp_rows, rows, cols, col_block)
     partial = lax.dot_general(
@@ -331,8 +404,15 @@
     coef = lax.optimization_barrier(coef).astype(jnp.bfloat16)
     coefs = exchange(jnp.broadcast_to(coef[None], (rows,) + coef.shape), "row")
 
-    outs = interpolate(counts, lists, node_data, centre_data, coefs)
-    summed = jnp.sum(exchange(outs, "col").astype(jnp.float32), axis=0)
+    parity = (lax.axis_index("col") % 2).astype(jnp.int32).reshape(1)
+    own, other = interpolate(parity, counts, lists, node_data, centre_data, coefs)
+    other = lax.ppermute(other, "col", [(c, c ^ 1) for c in range(cols)])
+    both = (own.astype(jnp.float32) + other.astype(jnp.float32)).astype(jnp.bfloat16)
+    chips = [[c for c in range(cols) if c % 2 == core] for core in range(2)]
+    both = lax.all_to_all(
+        both, "col", split_axis=0, concat_axis=0, axis_index_groups=chips, tiled=True
+    )
+    summed = jnp.sum(both.astype(jnp.float32), axis=0)
     ordered = jnp.concatenate([summed[:, :disp_rows], summed[:, 64 : 64 + disp_rows]], axis=0)
     return lax.dot_general(
         ordered.astype(jnp.bfloat16),

time: 198 us -> 193 us (0.975)
  blocking collectives: 28 us -> 17.3 us
  waiting for transfers between devices: 27.9 us -> 30.7 us
    all_to_all x1, blocking collectives: 28 us -> 17.3 us  [per_device(): lax.all_to_all(both, 'col', split_axis=0, concat_axis=0, axis_index_group...]
    ppermute x0 -> x1, waiting for transfers between devices: none -> 2.87 us  [per_device(): other = lax.ppermute(other, 'col', [(c, c ^ 1) for c in range(cols)])]
    convert_element_type x1 -> x2, other arithmetic: 4.13 us -> 5.63 us  [the longest x1 4.13 us: listed_groups(): jnp.where(minor, d[None, :, None], 0).astype(jnp.bfloat16)]
  transfers between devices with their start and end apart: 5 -> 6, of which waited for: 5 -> 6; matrix products, arithmetic and copies ran while one was open for 10% -> 10% of each run, Pallas kernels for 0% -> 0%
where the time goes in v2:
time: 193 us; the launch traced here: 192 us
  Pallas kernels  54.8 us (28%)
  waiting for transfers between devices  30.7 us (16%)
  starting transfers between devices  29.3 us (15%)
  matrix products  26.6 us (14%)
  other arithmetic  18.5 us (10%)
  blocking collectives  17.3 us (9%)
  local copies, waits for them, and re-layouts  13.8 us (7%)
    pallas_call x1, Pallas kernels, interpolate(): pl.pallas_call(kernel, out_shape=(out, out), in_specs=[smem, smem, smem,...  54.8 us
    all_to_all x5, starting transfers between devices, exchange(): return lax.all_to_all(value, axes, split_axis=0, concat_axis=0, tiled=True)  29.3 us
    all_to_all x5, waiting for transfers between devices, exchange(): return lax.all_to_all(value, axes, split_axis=0, concat_axis=0, tiled=True)  27.9 us
    all_to_all x1, blocking collectives, per_device(): lax.all_to_all(both, 'col', split_axis=0, concat_axis=0, axis_index_group...  17.3 us
    dot_general x1, matrix products, per_device(): jnp.dot(partial.astype(jnp.bfloat16), centre_pick, preferred_element_type...  12.1 us
    dot_general x2, matrix products, column_displacements(): lax.dot_general(part[:, :, :disp_rows], place, (((1,), (1,)), ((0,), (0,)...  4.71 us
    dot_general x1, matrix products, per_device(): lax.dot_general(ordered.astype(jnp.bfloat16), node_pick, (((0,), (1,)), (...  4.24 us
    convert_element_type x1, other arithmetic, listed_groups(): jnp.where(minor, d[None, :, None], 0).astype(jnp.bfloat16)  4.13 us
  transfers between devices with their start and end apart: 6, of which 6 were waited for; matrix products, arithmetic and copies ran while one was open for 10% of the time, Pallas kernels for 0%

profile of v2, /device:TPU:1, one launch (start us, length us, event | category | flops | bytes accessed | tf_op | source)
XLA Modules:
  0.0 191.6 jit_solution(5515287668422591821)
XLA Ops:
  0.0 0.8 multiply_add_fusion
  0.9 0.8 convert_element_type.118
  2.3 1.2 broadcast_in_dim.170
  3.5 0.8 convert_clamp_fusion
  4.3 0.8 reduce-precision_convert_fusion.1
  5.6 1.7 convert_reduce_fusion.1
  8.8 8.6 %all-to-all-start = ((f32[16,4,256]{2,1,0:T(4,128)}), f32[16,4,256]{2,1,0:T(4,128)S(1)}, u32[]{:S(2)}, u32[]{:S(2)}) async-start(f32[16,4,256]{2,1,0:T(4,128)} %broadcast_in_dim.188), calls=%async_computation | async-start | bytes 131072 | tf_op jit(solution)/shard_map/all_to_all | solution.py:31
  17.9 1.7 convert_reduce_fusion
  19.6 3.0 %fusion.1 = f32[9,2048]{1,0:T(8,128)S(1)} fusion(s32[2048]{0:T(1024)S(1)} %convert_reduce_fusion, bf16[3,2048]{1,0:T(4,128)(2,1)S(1)} %get-tuple-element.62, bf16[3,2048]{1,0:T(4,128)(2,1)S(1)} %get-tuple-element.64, bf16[3,2048]{1,0:T(4,128)(2,1)S(1)} %get-tuple-element.60), kind=kOutput, calls=%fused_computation.3 | convolution fusion | flops 79802368 | bytes 118784 | tf_op jit(solution)/shard_map/dot_general | solution.py:125
  23.9 0.7 broadcast_in_dim.190
  24.6 6.4 %all-to-all-start.1 = ((f32[8,4,2048]{2,1,0:T(4,128)}), f32[8,4,2048]{2,1,0:T(4,128)S(1)}, u32[]{:S(2)}, u32[]{:S(2)}) async-start(f32[8,4,2048]{2,1,0:T(4,128)} %broadcast_in_dim.190), calls=%async_computation.1 | async-start | bytes 524288 | tf_op jit(solution)/shard_map/all_to_all | solution.py:31
  33.4 4.1 %all-to-all-done.1.node_ref = f32[8,4,2048]{2,1,0:T(4,128)S(1)} async-done(((f32[8,4,2048]{2,1,0:T(4,128)}), f32[8,4,2048]{2,1,0:T(4,128)S(1)}, u32[]{:S(2)}, u32[]{:S(2)}) %all-to-all-start.1) | async-done | bytes 262176 | tf_op jit(solution)/shard_map/all_to_all | solution.py:31
  37.5 6.5 %all-to-all-start.2 = ((bf16[128,32,128]{2,1,0:T(8,128)(2,1)}), bf16[128,32,128]{2,1,0:T(8,128)(2,1)S(1)}, u32[]{:S(2)}, u32[]{:S(2)}) async-start(bf16[128,32,128]{2,1,0:T(8,128)(2,1)} %bitcast.1), calls=%async_computation.2 | async-start | bytes 2097152 | tf_op jit(solution)/shard_map/all_to_all | solution.py:31
  44.2 3.2 %add_reduce_fusion = f32[4,2,4,2048]{3,2,1,0:T(4,128)S(1)} fusion(f32[4,4,2,4,2]{3,4,2,1,0:T(2,128)S(1)} %copy.93, f32[2048]{0:T(1024)S(1)} %bitcast.107, f32[2048]{0:T(1024)S(1)} %bitcast.108, f32[4,4,2,4,2]{3,4,2,1,0:T(2,128)S(1)} %copy.91, f32[4,4,2,4,2]{3,4,2,1,0:T(2,128)S(1)} %copy.89, f32[2048]{0:T(1024)S(1)} %bitcast.109, f32[2048]{0:T(1024)S(1)} %bitcast.110, ...), kind=kLoop, calls=%fused_computation.24 | loop fusion | flops 9371648 | bytes 317440 | tf_op jit(solution)/shard_map/reduce_min | solution.py:153
  48.8 4.1 %select_convert_fusion.1 = (bf16[8,2048,128]{2,1,0:T(8,128)(2,1)S(1)}, bf16[8,2048,128]{2,1,0:T(8,128)(2,1)S(1)}) fusion(s32[2048]{0:T(1024)S(1)} %get-tuple-element.97, s32[8,2048]{1,0:T(8,128)S(1)} %add_select_fusion, s32[2048]{0:T(1024)S(1)} %get-tuple-element.96), kind=kLoop, calls=%fused_computation.13 | loop fusion | flops 10485760 | bytes 8470528 | tf_op jit(solution)/shard_map/convert_element_type | solution.py:178
  52.9 1.6 fusion.3
  54.5 8.8 %all-to-all-done.2 = bf16[128,32,128]{2,1,0:T(8,128)(2,1)S(1)} async-done(((bf16[128,32,128]{2,1,0:T(8,128)(2,1)}), bf16[128,32,128]{2,1,0:T(8,128)(2,1)S(1)}, u32[]{:S(2)}, u32[]{:S(2)}) %all-to-all-start.2) | async-done | bytes 1048608 | tf_op jit(solution)/shard_map/all_to_all | solution.py:31
  65.0 1.7 fusion.126
  68.2 2.4 %fusion.17 = bf16[8,48,256]{2,1,0:T(8,128)(2,1)S(1)} fusion(bf16[8,512,48]{2,0,1:T(8,128)(2,1)} %get-tuple-element.34, bf16[256]{0:T(256)(128)(2,1)S(1)} %iota_convert_fusion, bf16[8,512]{1,0:T(8,128)(2,1)S(1)} %bitcast.126), kind=kOutput, calls=%fused_computation.27 | convolution fusion | flops 101810176 | bytes 598528 | tf_op jit(solution)/shard_map/dot_general | solution.py:74
  70.5 2.4 %fusion.20 = bf16[8,48,256]{2,1,0:T(8,128)(2,1)S(1)} fusion(bf16[8,512,48]{2,0,1:T(8,128)(2,1)} %get-tuple-element.35, bf16[8,512]{1,0:T(8,128)(2,1)S(1)} %bitcast.125, bf16[256]{0:T(256)(128)(2,1)S(1)} %iota_convert_fusion), kind=kOutput, calls=%fused_computation.28 | convolution fusion | flops 101810176 | bytes 598528 | tf_op jit(solution)/shard_map/dot_general | solution.py:74
  73.0 12.1 %fusion.14 = bf16[48,2048]{1,0:T(8,128)(2,1)S(1)} fusion(s32[2048]{0:T(1024)S(1)} %fusion.73, bf16[48,4096]{1,0:T(8,128)(2,1)S(1)} %bitcast.99, bf16[2048,4096]{1,0:T(8,128)(2,1)} %param.7), kind=kOutput, calls=%fused_computation.21 | convolution fusion | flops 1212350464 | bytes 17375232 | tf_op jit(solution)/shard_map/dot_general | solution.py:400
  85.8 4.3 %all-to-all-start.3 = ((bf16[8,48,256]{2,1,0:T(8,128)(2,1)}), bf16[8,48,256]{2,1,0:T(8,128)(2,1)S(1)}, u32[]{:S(2)}, u32[]{:S(2)}) async-start(bf16[8,48,256]{2,1,0:T(8,128)(2,1)} %bitcast.92), calls=%async_computation.3 | async-start | bytes 393216 | tf_op jit(solution)/shard_map/all_to_all | solution.py:31
  90.1 5.8 %all-to-all-done.3 = bf16[8,48,256]{2,1,0:T(8,128)(2,1)S(1)} async-done(((bf16[8,48,256]{2,1,0:T(8,128)(2,1)}), bf16[8,48,256]{2,1,0:T(8,128)(2,1)S(1)}, u32[]{:S(2)}, u32[]{:S(2)}) %all-to-all-start.3) | async-done | bytes 196640 | tf_op jit(solution)/shard_map/all_to_all | solution.py:31
  96.0 0.8 broadcast_in_dim.199
  96.8 3.6 %all-to-all-start.4 = ((bf16[16,48,256]{2,1,0:T(8,128)(2,1)}), bf16[16,48,256]{2,1,0:T(8,128)(2,1)S(1)}, u32[]{:S(2)}, u32[]{:S(2)}) async-start(bf16[16,48,256]{2,1,0:T(8,128)(2,1)} %broadcast_in_dim.199), calls=%async_computation.4 | async-start | bytes 786432 | tf_op jit(solution)/shard_map/all_to_all | solution.py:31
  101.0 8.5 %all-to-all-done.4.coef_ref = bf16[16,48,256]{2,1,0:T(8,128)(2,1)S(1)} async-done(((bf16[16,48,256]{2,1,0:T(8,128)(2,1)}), bf16[16,48,256]{2,1,0:T(8,128)(2,1)S(1)}, u32[]{:S(2)}, u32[]{:S(2)}) %all-to-all-start.4) | async-done | bytes 393248 | tf_op jit(solution)/shard_map/all_to_all | solution.py:31
  109.5 0.7 copy-done.1
  110.3 54.8 %interpolate.1 = (bf16[4,1024,128]{2,1,0:T(8,128)(2,1)}, bf16[4,1024,128]{2,1,0:T(8,128)(2,1)}) custom-call(s32[1]{0:T(128)} %bitcast.parity_ref, s32[8]{0:T(128)} %bitcast.130, s32[8,2080]{1,0:T(8,128)} %pad_select_fusion.list_ref, f32[8,4,2048]{2,1,0:T(4,128)} %copy-done.2, f32[16,4,256]{2,1,0:T(4,128)} %copy-done.3, bf16[16,48,256]{2,1,0:T(8,128)(2,1)} %copy-done.1), custom_call_target="tpu_custom_call" | custom-call | tf_op jit(solution)/shard_map/interpolate/pallas_call | solution.py:344
  165.1 2.9 %collective-permute-done = bf16[4,1024,128]{2,1,0:T(8,128)(2,1)S(1)} collective-permute-done((bf16[4,1024,128]{2,1,0:T(8,128)(2,1)}, bf16[4,1024,128]{2,1,0:T(8,128)(2,1)S(1)}, u32[]{:S(2)}, u32[]{:S(2)}) %collective-permute-start) | collective-permute-done | bytes 1048608 | tf_op jit(solution)/shard_map/ppermute | solution.py:409
  167.9 1.5 add_convert_fusion
  169.4 17.3 %all_to_all.30 = bf16[4,1024,128]{2,1,0:T(8,128)(2,1)S(1)} all-to-all(bf16[4,1024,128]{2,1,0:T(8,128)(2,1)S(1)} %add_convert_fusion), channel_id=1, replica_groups={{0,2,4,6},{1,3,5,7},{8,10,12,14},{9,11,13,15},{16,18,20,22},{17,19,21,2..., dimensions={0} | all-to-all | bytes 2097152 | tf_op jit(solution)/shard_map/all_to_all | solution.py:412
  187.4 4.2 %fusion = f32[48,2048]{1,0:T(8,128)} fusion(s32[2048]{0:T(1024)S(1)} %convert_reduce_fusion, bf16[1024,48]{0,1:T(8,128)(2,1)S(1)} %copy.104, bf16[1024,48]{0,1:T(8,128)(2,1)S(1)} %copy.103), kind=kOutput, calls=%fused_computation.2 | convolution fusion | flops 407240704 | bytes 598016 | tf_op jit(solution)/shard_map/dot_general | solution.py:417
  (118 shorter events, 13.2 us)
Async XLA Ops:
  0.0 2.2 %copy-start = (f32[3,32768]{1,0:T(4,128)S(1)}, f32[3,32768]{1,0:T(4,128)}, u32[]{:S(2)}) copy-start(f32[3,32768]{1,0:T(4,128)} %param.8) | copy-start | bytes 1179652
  8.8 15.1 %all-to-all-start = ((f32[16,4,256]{2,1,0:T(4,128)}), f32[16,4,256]{2,1,0:T(4,128)S(1)}, u32[]{:S(2)}, u32[]{:S(2)}) async-start(f32[16,4,256]{2,1,0:T(4,128)} %broadcast_in_dim.188), calls=%async_computation | async-start | bytes 131072 | tf_op jit(solution)/shard_map/all_to_all | solution.py:31
  23.9 29.0 %copy-start.3 = (f32[16,4,256]{2,1,0:T(4,128)}, f32[16,4,256]{2,1,0:T(4,128)S(1)}, u32[]{:S(2)}) copy-start(f32[16,4,256]{2,1,0:T(4,128)S(1)} %all-to-all-done.centre_ref) | copy-start | bytes 196612
  24.6 12.9 %all-to-all-start.1 = ((f32[8,4,2048]{2,1,0:T(4,128)}), f32[8,4,2048]{2,1,0:T(4,128)S(1)}, u32[]{:S(2)}, u32[]{:S(2)}) async-start(f32[8,4,2048]{2,1,0:T(4,128)} %broadcast_in_dim.190), calls=%async_computation.1 | async-start | bytes 524288 | tf_op jit(solution)/shard_map/all_to_all | solution.py:31
  37.5 15.4 %copy-start.2 = (f32[8,4,2048]{2,1,0:T(4,128)}, f32[8,4,2048]{2,1,0:T(4,128)S(1)}, u32[]{:S(2)}) copy-start(f32[8,4,2048]{2,1,0:T(4,128)S(1)} %all-to-all-done.1.node_ref) | copy-start | bytes 786436
  37.5 25.8 %all-to-all-start.2 = ((bf16[128,32,128]{2,1,0:T(8,128)(2,1)}), bf16[128,32,128]{2,1,0:T(8,128)(2,1)S(1)}, u32[]{:S(2)}, u32[]{:S(2)}) async-start(bf16[128,32,128]{2,1,0:T(8,128)(2,1)} %bitcast.1), calls=%async_computation.2 | async-start | bytes 2097152 | tf_op jit(solution)/shard_map/all_to_all | solution.py:31
  48.7 51.6 %copy-start.4 = (s32[8,1]{0,1:T(1,128)}, s32[8,1]{0,1:T(1,128)S(1)}, u32[]{:S(2)}) copy-start(s32[8,1]{0,1:T(1,128)S(1)} %copy.119) | copy-start | bytes 100
  85.8 10.1 %all-to-all-start.3 = ((bf16[8,48,256]{2,1,0:T(8,128)(2,1)}), bf16[8,48,256]{2,1,0:T(8,128)(2,1)S(1)}, u32[]{:S(2)}, u32[]{:S(2)}) async-start(bf16[8,48,256]{2,1,0:T(8,128)(2,1)} %bitcast.92), calls=%async_computation.3 | async-start | bytes 393216 | tf_op jit(solution)/shard_map/all_to_all | solution.py:31
  96.8 12.8 %all-to-all-start.4 = ((bf16[16,48,256]{2,1,0:T(8,128)(2,1)}), bf16[16,48,256]{2,1,0:T(8,128)(2,1)S(1)}, u32[]{:S(2)}, u32[]{:S(2)}) async-start(bf16[16,48,256]{2,1,0:T(8,128)(2,1)} %broadcast_in_dim.199), calls=%async_computation.4 | async-start | bytes 786432 | tf_op jit(solution)/shard_map/all_to_all | solution.py:31
  109.5 0.7 copy-start.1
  165.1 2.9 %collective-permute-start = (bf16[4,1024,128]{2,1,0:T(8,128)(2,1)}, bf16[4,1024,128]{2,1,0:T(8,128)(2,1)S(1)}, u32[]{:S(2)}, u32[]{:S(2)}) collective-permute-start(bf16[4,1024,128]{2,1,0:T(8,128)(2,1)} %get-tuple-element.14), channel_id=1, source_target_pairs={{0,1},{1,0},{2,3},{3,2},{4,5},{5,4},{6,7},{7,6},{8,9},{9,8},{10,11... | collective-permute-start | bytes 3145736 | tf_op jit(solution)/shard_map/ppermute | solution.py:409

commit v3 on v2

--- a/solution.py
+++ b/solution.py
@@ -185,7 +185,7 @@
     listed = (listed[:, :, :LANES] * 64.0 + listed[:, :, LANES:]).reshape(blocks, total)
     listed = jnp.pad(listed.astype(jnp.int32), ((0, 0), (0, BATCH)))
     slots = jnp.arange(total + BATCH, dtype=jnp.int32)
-    return counts, jnp.where(slots[None, :] < counts[:, None], listed, total)
+    return counts, jnp.where(slots[None, :] < counts[:, None], listed, total) * GROUP
 
 
 def interpolate(parity, counts, lists, node_data, centre_data, coefs):
@@ -218,6 +218,7 @@
         table_ref,
     ):
         acc_ref[total:, :] = jnp.zeros((GROUP, LANES), jnp.float32)
+        row_ref[total:, :] = jnp.zeros((GROUP, 8), jnp.float32)
         for col in range(cols):
 
             def prepare(step, carry):
@@ -228,7 +229,7 @@
                 acc_ref[pl.ds(col * nodes + first, LANES), :] = jnp.zeros((LANES, LANES), jnp.float32)
                 return carry
 
-            lax.fori_loop(0, nodes // LANES, prepare, 0)
+            lax.fori_loop(0, nodes // LANES, prepare, 0, unroll=4)
 
         lane = lax.broadcasted_iota(jnp.int32, (1, LANES), 1)
         segment = lane // BLOCK
@@ -263,17 +264,14 @@
         for extra in range(3):
             fill(number + extra, 0, last)
 
-        def ids(place):
+        def starts(place):
             block = table_ref[0, place]
             start = table_ref[1, place]
             return [list_ref[block, start + i] for i in range(BATCH)]
 
         def spread(place, spread_ref):
             node = jnp.concatenate(
-                [
-                    row_ref[pl.ds(pl.multiple_of(jnp.minimum(i, last - 1) * GROUP, GROUP), GROUP), :]
-                    for i in ids(place)
-                ],
+                [row_ref[pl.ds(pl.multiple_of(start, GROUP), GROUP), :] for start in starts(place)],
                 axis=0,
             )
             for axis in range(3):
@@ -304,9 +302,10 @@
                 (((1,), (1,)), ((), ())),
                 preferred_element_type=jnp.float32,
             )
-            for i, group in enumerate(ids(place)):
-                start = pl.multiple_of(group * GROUP, GROUP)
-                acc_ref[pl.ds(start, GROUP), :disp_rows] += part[i * GROUP : (i + 1) * GROUP]
+            places = [pl.ds(pl.multiple_of(start, GROUP), GROUP) for start in starts(place)]
+            before = [acc_ref[rows_of, :disp_rows] for rows_of in places]
+            for i, rows_of in enumerate(places):
+                acc_ref[rows_of, :disp_rows] = before[i] + part[i * GROUP : (i + 1) * GROUP]
 
         spread(1, spread_0)
 
@@ -336,7 +335,7 @@
                     out_ref[chip, pl.ds(first, LANES), :] = (both * (1.0 / 256.0)).astype(jnp.bfloat16)
                     return carry
 
-                lax.fori_loop(0, nodes // 2 // LANES, pack, 0)
+                lax.fori_loop(0, nodes // 2 // LANES, pack, 0, unroll=4)
 
     vmem = pl.BlockSpec(memory_space=pltpu.VMEM)
     smem = pl.BlockSpec(memory_space=pltpu.SMEM)
@@ -348,7 +347,7 @@
         out_specs=(vmem, vmem),
         scratch_shapes=[
             pltpu.VMEM((total + GROUP, LANES), jnp.float32),
-            pltpu.VMEM((total, 8), jnp.float32),
+            pltpu.VMEM((total + GROUP, 8), jnp.float32),
             pltpu.VMEM((16 * blocks, LANES), jnp.float32),
             pltpu.VMEM((blocks, disp_rows, quads * LANES), jnp.bfloat16),
             pltpu.VMEM((size, quads * LANES), jnp.bfloat16),
@@ -376,8 +375,10 @@
     recv = exchange(send, ("row", "col"))
 
     rank = sorted_rank(own_xyz)
-    turn = (rank // BLOCK + row_index) % (LANES // BLOCK)
-    centre_slot = rank // LANES * LANES + turn * BLOCK + rank % BLOCK
+    block = rank // BLOCK
+    turns = LANES // BLOCK
+    place = block // cols
+    centre_slot = block % cols * piece + place // turns * LANES + (place + row_index) % turns * BLOCK + rank % BLOCK
     order = jnp.arange(row_block, dtype=jnp.int32)
     centre_pick = (centre_slot[:, None] == order[None, :]).astype(jnp.bfloat16)
     piece_order = lax.axis_index("col") * piece + jnp.arange(piece, dtype=jnp.int32)

time: 193 us -> 174 us (0.902)
  Pallas kernels: 54.8 us -> 33.4 us
  starting transfers between devices: 29.3 us -> 32 us
    pallas_call x1, Pallas kernels: 54.8 us -> 33.4 us  [interpolate(): pl.pallas_call(kernel, out_shape=(out, out), in_specs=[smem, smem, smem,...]
    ppermute x1, starting transfers between devices: 0.01 us -> 2.68 us  [per_device(): other = lax.ppermute(other, 'col', [(c, c ^ 1) for c in range(cols)])]
  transfers between devices with their start and end apart: 6 -> 6, of which waited for: 6 -> 6; matrix products, arithmetic and copies ran while one was open for 10% -> 11% of each run, Pallas kernels for 0% -> 0%
where the time goes in v3:
time: 174 us; the launch traced here: 173 us
  Pallas kernels  33.4 us (19%)
  starting transfers between devices  32 us (18%)
  waiting for transfers between devices  30.4 us (17%)
  matrix products  26.6 us (15%)
  other arithmetic  18.5 us (11%)
  blocking collectives  17.4 us (10%)
  local copies, waits for them, and re-layouts  13.8 us (8%)
    pallas_call x1, Pallas kernels, interpolate(): pl.pallas_call(kernel, out_shape=(out, out), in_specs=[smem, smem, smem,...  33.4 us
    all_to_all x5, starting transfers between devices, exchange(): return lax.all_to_all(value, axes, split_axis=0, concat_axis=0, tiled=True)  29.3 us
    all_to_all x5, waiting for transfers between devices, exchange(): return lax.all_to_all(value, axes, split_axis=0, concat_axis=0, tiled=True)  27.9 us
    all_to_all x1, blocking collectives, per_device(): lax.all_to_all(both, 'col', split_axis=0, concat_axis=0, axis_index_group...  17.4 us
    dot_general x1, matrix products, per_device(): jnp.dot(partial.astype(jnp.bfloat16), centre_pick, preferred_element_type...  12.1 us
    dot_general x2, matrix products, column_displacements(): lax.dot_general(part[:, :, :disp_rows], place, (((1,), (1,)), ((0,), (0,)...  4.71 us
    dot_general x1, matrix products, per_device(): lax.dot_general(ordered.astype(jnp.bfloat16), node_pick, (((0,), (1,)), (...  4.24 us
    convert_element_type x1, other arithmetic, listed_groups(): jnp.where(minor, d[None, :, None], 0).astype(jnp.bfloat16)  4.13 us
  transfers between devices with their start and end apart: 6, of which 6 were waited for; matrix products, arithmetic and copies ran while one was open for 11% of the time, Pallas kernels for 0%

profile of v3, /device:TPU:1, one launch (start us, length us, event | category | flops | bytes accessed | tf_op | source)
XLA Modules:
  0.0 172.7 jit_solution(17717876138182167404)
XLA Ops:
  0.0 0.8 multiply_add_fusion
  0.9 0.8 convert_element_type.118
  2.3 1.2 broadcast_in_dim.170
  3.5 0.8 convert_clamp_fusion
  4.3 0.8 reduce-precision_convert_fusion.1
  5.6 1.7 convert_reduce_fusion.1
  8.8 8.6 %all-to-all-start = ((f32[16,4,256]{2,1,0:T(4,128)}), f32[16,4,256]{2,1,0:T(4,128)S(1)}, u32[]{:S(2)}, u32[]{:S(2)}) async-start(f32[16,4,256]{2,1,0:T(4,128)} %broadcast_in_dim.188), calls=%async_computation | async-start | bytes 131072 | tf_op jit(solution)/shard_map/all_to_all | solution.py:31
  17.9 1.7 convert_reduce_fusion
  19.6 3.0 %fusion.1 = f32[9,2048]{1,0:T(8,128)S(1)} fusion(s32[2048]{0:T(1024)S(1)} %convert_reduce_fusion, bf16[3,2048]{1,0:T(4,128)(2,1)S(1)} %get-tuple-element.62, bf16[3,2048]{1,0:T(4,128)(2,1)S(1)} %get-tuple-element.64, bf16[3,2048]{1,0:T(4,128)(2,1)S(1)} %get-tuple-element.60), kind=kOutput, calls=%fused_computation.3 | convolution fusion | flops 79802368 | bytes 118784 | tf_op jit(solution)/shard_map/dot_general | solution.py:125
  24.7 6.4 %all-to-all-start.1 = ((f32[8,4,2048]{2,1,0:T(4,128)}), f32[8,4,2048]{2,1,0:T(4,128)S(1)}, u32[]{:S(2)}, u32[]{:S(2)}) async-start(f32[8,4,2048]{2,1,0:T(4,128)} %broadcast_in_dim.190), calls=%async_computation.1 | async-start | bytes 524288 | tf_op jit(solution)/shard_map/all_to_all | solution.py:31
  33.4 4.1 %all-to-all-done.1.node_ref = f32[8,4,2048]{2,1,0:T(4,128)S(1)} async-done(((f32[8,4,2048]{2,1,0:T(4,128)}), f32[8,4,2048]{2,1,0:T(4,128)S(1)}, u32[]{:S(2)}, u32[]{:S(2)}) %all-to-all-start.1) | async-done | bytes 262176 | tf_op jit(solution)/shard_map/all_to_all | solution.py:31
  37.5 6.5 %all-to-all-start.2 = ((bf16[128,32,128]{2,1,0:T(8,128)(2,1)}), bf16[128,32,128]{2,1,0:T(8,128)(2,1)S(1)}, u32[]{:S(2)}, u32[]{:S(2)}) async-start(bf16[128,32,128]{2,1,0:T(8,128)(2,1)} %bitcast.1), calls=%async_computation.2 | async-start | bytes 2097152 | tf_op jit(solution)/shard_map/all_to_all | solution.py:31
  44.2 3.2 %add_reduce_fusion = f32[4,2,4,2048]{3,2,1,0:T(4,128)S(1)} fusion(f32[4,4,2,4,2]{3,4,2,1,0:T(2,128)S(1)} %copy.93, f32[2048]{0:T(1024)S(1)} %bitcast.107, f32[2048]{0:T(1024)S(1)} %bitcast.108, f32[4,4,2,4,2]{3,4,2,1,0:T(2,128)S(1)} %copy.91, f32[4,4,2,4,2]{3,4,2,1,0:T(2,128)S(1)} %copy.89, f32[2048]{0:T(1024)S(1)} %bitcast.109, f32[2048]{0:T(1024)S(1)} %bitcast.110, ...), kind=kLoop, calls=%fused_computation.24 | loop fusion | flops 9371648 | bytes 317440 | tf_op jit(solution)/shard_map/reduce_min | solution.py:153
  48.8 4.1 %select_convert_fusion.1 = (bf16[8,2048,128]{2,1,0:T(8,128)(2,1)S(1)}, bf16[8,2048,128]{2,1,0:T(8,128)(2,1)S(1)}) fusion(s32[2048]{0:T(1024)S(1)} %get-tuple-element.97, s32[8,2048]{1,0:T(8,128)S(1)} %add_select_fusion, s32[2048]{0:T(1024)S(1)} %get-tuple-element.96), kind=kLoop, calls=%fused_computation.13 | loop fusion | flops 10485760 | bytes 8470528 | tf_op jit(solution)/shard_map/convert_element_type | solution.py:178
  52.9 1.6 fusion.3
  54.5 8.8 %all-to-all-done.2 = bf16[128,32,128]{2,1,0:T(8,128)(2,1)S(1)} async-done(((bf16[128,32,128]{2,1,0:T(8,128)(2,1)}), bf16[128,32,128]{2,1,0:T(8,128)(2,1)S(1)}, u32[]{:S(2)}, u32[]{:S(2)}) %all-to-all-start.2) | async-done | bytes 1048608 | tf_op jit(solution)/shard_map/all_to_all | solution.py:31
  65.0 1.7 %fusion.130 = (bf16[8,512,48]{2,0,1:T(8,128)(2,1)}, bf16[8,512,48]{2,0,1:T(8,128)(2,1)}) fusion(bf16[8,512,128]{2,0,1:T(8,128)(2,1)S(1)} %bitcast.97), kind=kLoop, calls=%fused_computation.342 | loop fusion | bytes 1572864 | tf_op jit(solution)/shard_map/slice | solution.py:75
  68.2 2.4 %fusion.17 = bf16[8,48,256]{2,1,0:T(8,128)(2,1)S(1)} fusion(bf16[8,512,48]{2,0,1:T(8,128)(2,1)} %get-tuple-element.34, bf16[256]{0:T(256)(128)(2,1)S(1)} %iota_convert_fusion, bf16[8,512]{1,0:T(8,128)(2,1)S(1)} %bitcast.126), kind=kOutput, calls=%fused_computation.27 | convolution fusion | flops 101810176 | bytes 598528 | tf_op jit(solution)/shard_map/dot_general | solution.py:74
  70.6 2.4 %fusion.20 = bf16[8,48,256]{2,1,0:T(8,128)(2,1)S(1)} fusion(bf16[8,512,48]{2,0,1:T(8,128)(2,1)} %get-tuple-element.35, bf16[8,512]{1,0:T(8,128)(2,1)S(1)} %bitcast.125, bf16[256]{0:T(256)(128)(2,1)S(1)} %iota_convert_fusion), kind=kOutput, calls=%fused_computation.28 | convolution fusion | flops 101810176 | bytes 598528 | tf_op jit(solution)/shard_map/dot_general | solution.py:74
  73.0 12.1 %fusion.14 = bf16[48,2048]{1,0:T(8,128)(2,1)S(1)} fusion(s32[2048]{0:T(1024)S(1)} %fusion.73, bf16[48,4096]{1,0:T(8,128)(2,1)S(1)} %bitcast.99, bf16[2048,4096]{1,0:T(8,128)(2,1)} %param.7), kind=kOutput, calls=%fused_computation.21 | convolution fusion | flops 1212350464 | bytes 17375232 | tf_op jit(solution)/shard_map/dot_general | solution.py:401
  85.8 4.3 %all-to-all-start.3 = ((bf16[8,48,256]{2,1,0:T(8,128)(2,1)}), bf16[8,48,256]{2,1,0:T(8,128)(2,1)S(1)}, u32[]{:S(2)}, u32[]{:S(2)}) async-start(bf16[8,48,256]{2,1,0:T(8,128)(2,1)} %bitcast.92), calls=%async_computation.3 | async-start | bytes 393216 | tf_op jit(solution)/shard_map/all_to_all | solution.py:31
  90.1 5.8 %all-to-all-done.3 = bf16[8,48,256]{2,1,0:T(8,128)(2,1)S(1)} async-done(((bf16[8,48,256]{2,1,0:T(8,128)(2,1)}), bf16[8,48,256]{2,1,0:T(8,128)(2,1)S(1)}, u32[]{:S(2)}, u32[]{:S(2)}) %all-to-all-start.3) | async-done | bytes 196640 | tf_op jit(solution)/shard_map/all_to_all | solution.py:31
  96.0 0.8 broadcast_in_dim.199
  96.8 3.6 %all-to-all-start.4 = ((bf16[16,48,256]{2,1,0:T(8,128)(2,1)}), bf16[16,48,256]{2,1,0:T(8,128)(2,1)S(1)}, u32[]{:S(2)}, u32[]{:S(2)}) async-start(bf16[16,48,256]{2,1,0:T(8,128)(2,1)} %broadcast_in_dim.199), calls=%async_computation.4 | async-start | bytes 786432 | tf_op jit(solution)/shard_map/all_to_all | solution.py:31
  101.0 8.5 %all-to-all-done.4.coef_ref = bf16[16,48,256]{2,1,0:T(8,128)(2,1)S(1)} async-done(((bf16[16,48,256]{2,1,0:T(8,128)(2,1)}), bf16[16,48,256]{2,1,0:T(8,128)(2,1)S(1)}, u32[]{:S(2)}, u32[]{:S(2)}) %all-to-all-start.4) | async-done | bytes 393248 | tf_op jit(solution)/shard_map/all_to_all | solution.py:31
  109.5 0.7 copy-done.1
  110.3 33.4 %interpolate.1 = (bf16[4,1024,128]{2,1,0:T(8,128)(2,1)}, bf16[4,1024,128]{2,1,0:T(8,128)(2,1)}) custom-call(s32[1]{0:T(128)} %bitcast.parity_ref, s32[8]{0:T(128)} %bitcast.130, s32[8,2080]{1,0:T(8,128)} %select_multiply_fusion.list_ref, f32[8,4,2048]{2,1,0:T(4,128)} %copy-done.2, f32[16,4,256]{2,1,0:T(4,128)} %copy-done.3, bf16[16,48,256]{2,1,0:T(8,128)(2,1)} %copy-done.1), custom_call_target="tpu_custom_call" | custom-call | tf_op jit(solution)/shard_map/interpolate/pallas_call | solution.py:343
  143.7 2.7 %collective-permute-start = (bf16[4,1024,128]{2,1,0:T(8,128)(2,1)}, bf16[4,1024,128]{2,1,0:T(8,128)(2,1)S(1)}, u32[]{:S(2)}, u32[]{:S(2)}) collective-permute-start(bf16[4,1024,128]{2,1,0:T(8,128)(2,1)} %get-tuple-element.14), channel_id=1, source_target_pairs={{0,1},{1,0},{2,3},{3,2},{4,5},{5,4},{6,7},{7,6},{8,9},{9,8},{10,11... | collective-permute-start | bytes 3145736 | tf_op jit(solution)/shard_map/ppermute | solution.py:410
  146.4 2.5 %collective-permute-done = bf16[4,1024,128]{2,1,0:T(8,128)(2,1)S(1)} collective-permute-done((bf16[4,1024,128]{2,1,0:T(8,128)(2,1)}, bf16[4,1024,128]{2,1,0:T(8,128)(2,1)S(1)}, u32[]{:S(2)}, u32[]{:S(2)}) %collective-permute-start) | collective-permute-done | bytes 1048608 | tf_op jit(solution)/shard_map/ppermute | solution.py:410
  148.9 1.5 add_convert_fusion
  150.4 17.4 %all_to_all.30 = bf16[4,1024,128]{2,1,0:T(8,128)(2,1)S(1)} all-to-all(bf16[4,1024,128]{2,1,0:T(8,128)(2,1)S(1)} %add_convert_fusion), channel_id=1, replica_groups={{0,2,4,6},{1,3,5,7},{8,10,12,14},{9,11,13,15},{16,18,20,22},{17,19,21,2..., dimensions={0} | all-to-all | bytes 2097152 | tf_op jit(solution)/shard_map/all_to_all | solution.py:413
  168.4 4.2 %fusion = f32[48,2048]{1,0:T(8,128)} fusion(s32[2048]{0:T(1024)S(1)} %convert_reduce_fusion, bf16[1024,48]{0,1:T(8,128)(2,1)S(1)} %copy.104, bf16[1024,48]{0,1:T(8,128)(2,1)S(1)} %copy.103), kind=kOutput, calls=%fused_computation.2 | convolution fusion | flops 407240704 | bytes 598016 | tf_op jit(solution)/shard_map/dot_general | solution.py:418
  (118 shorter events, 14.0 us)
Async XLA Ops:
  0.0 2.2 %copy-start = (f32[3,32768]{1,0:T(4,128)S(1)}, f32[3,32768]{1,0:T(4,128)}, u32[]{:S(2)}) copy-start(f32[3,32768]{1,0:T(4,128)} %param.8) | copy-start | bytes 1179652
  8.8 15.1 %all-to-all-start = ((f32[16,4,256]{2,1,0:T(4,128)}), f32[16,4,256]{2,1,0:T(4,128)S(1)}, u32[]{:S(2)}, u32[]{:S(2)}) async-start(f32[16,4,256]{2,1,0:T(4,128)} %broadcast_in_dim.188), calls=%async_computation | async-start | bytes 131072 | tf_op jit(solution)/shard_map/all_to_all | solution.py:31
  23.9 29.0 %copy-start.3 = (f32[16,4,256]{2,1,0:T(4,128)}, f32[16,4,256]{2,1,0:T(4,128)S(1)}, u32[]{:S(2)}) copy-start(f32[16,4,256]{2,1,0:T(4,128)S(1)} %all-to-all-done.centre_ref) | copy-start | bytes 196612
  24.7 12.9 %all-to-all-start.1 = ((f32[8,4,2048]{2,1,0:T(4,128)}), f32[8,4,2048]{2,1,0:T(4,128)S(1)}, u32[]{:S(2)}, u32[]{:S(2)}) async-start(f32[8,4,2048]{2,1,0:T(4,128)} %broadcast_in_dim.190), calls=%async_computation.1 | async-start | bytes 524288 | tf_op jit(solution)/shard_map/all_to_all | solution.py:31
  37.5 15.4 %copy-start.2 = (f32[8,4,2048]{2,1,0:T(4,128)}, f32[8,4,2048]{2,1,0:T(4,128)S(1)}, u32[]{:S(2)}) copy-start(f32[8,4,2048]{2,1,0:T(4,128)S(1)} %all-to-all-done.1.node_ref) | copy-start | bytes 786436
  37.5 25.8 %all-to-all-start.2 = ((bf16[128,32,128]{2,1,0:T(8,128)(2,1)}), bf16[128,32,128]{2,1,0:T(8,128)(2,1)S(1)}, u32[]{:S(2)}, u32[]{:S(2)}) async-start(bf16[128,32,128]{2,1,0:T(8,128)(2,1)} %bitcast.1), calls=%async_computation.2 | async-start | bytes 2097152 | tf_op jit(solution)/shard_map/all_to_all | solution.py:31
  48.8 51.6 %copy-start.4 = (s32[8,1]{0,1:T(1,128)}, s32[8,1]{0,1:T(1,128)S(1)}, u32[]{:S(2)}) copy-start(s32[8,1]{0,1:T(1,128)S(1)} %copy.119) | copy-start | bytes 100
  85.8 10.1 %all-to-all-start.3 = ((bf16[8,48,256]{2,1,0:T(8,128)(2,1)}), bf16[8,48,256]{2,1,0:T(8,128)(2,1)S(1)}, u32[]{:S(2)}, u32[]{:S(2)}) async-start(bf16[8,48,256]{2,1,0:T(8,128)(2,1)} %bitcast.92), calls=%async_computation.3 | async-start | bytes 393216 | tf_op jit(solution)/shard_map/all_to_all | solution.py:31
  96.8 12.8 %all-to-all-start.4 = ((bf16[16,48,256]{2,1,0:T(8,128)(2,1)}), bf16[16,48,256]{2,1,0:T(8,128)(2,1)S(1)}, u32[]{:S(2)}, u32[]{:S(2)}) async-start(bf16[16,48,256]{2,1,0:T(8,128)(2,1)} %broadcast_in_dim.199), calls=%async_computation.4 | async-start | bytes 786432 | tf_op jit(solution)/shard_map/all_to_all | solution.py:31
  109.5 0.7 copy-start.1
  143.7 5.2 %collective-permute-start = (bf16[4,1024,128]{2,1,0:T(8,128)(2,1)}, bf16[4,1024,128]{2,1,0:T(8,128)(2,1)S(1)}, u32[]{:S(2)}, u32[]{:S(2)}) collective-permute-start(bf16[4,1024,128]{2,1,0:T(8,128)(2,1)} %get-tuple-element.14), channel_id=1, source_target_pairs={{0,1},{1,0},{2,3},{3,2},{4,5},{5,4},{6,7},{7,6},{8,9},{9,8},{10,11... | collective-permute-start | bytes 3145736 | tf_op jit(solution)/shard_map/ppermute | solution.py:410

commit v4 on v3

--- a/solution.py
+++ b/solution.py
@@ -17,6 +17,8 @@
 LANES = 128
 BLOCK = 32
 BOX = 16
+PARTS = 8
+PACK = 64
 FACES = (
     (1, 0, (0, 0, 0), 0),
     (2, 0, (1, 0, 0), 0),
@@ -321,25 +323,38 @@
 
         lax.fori_loop(0, (number + 1) // 2, two, 0)
 
-        low_lanes = lane < LANES // 2
+        part_rows = nodes // PARTS
         for side, out_ref in enumerate((own_ref, other_ref)):
             for chip in range(cols // 2):
                 col = 2 * chip + (parity_ref[0] + side) % 2
 
                 def pack(step, carry):
-                    first = pl.multiple_of(step * LANES, LANES)
+                    first = pl.multiple_of(step * PACK, PACK)
                     start = pl.multiple_of(col * nodes, nodes) + first
-                    low = acc_ref[pl.ds(start, LANES), :]
-                    high = acc_ref[pl.ds(start + nodes // 2, LANES), :]
-                    both = jnp.where(low_lanes, low, pltpu.roll(high, LANES // 2, 1))
-                    out_ref[chip, pl.ds(first, LANES), :] = (both * (1.0 / 256.0)).astype(jnp.bfloat16)
+                    filled = [None] * (PARTS * disp_rows // LANES)
+                    for i in range(PARTS):
+                        value = acc_ref[pl.ds(start + i * part_rows, PACK), :]
+                        shift = i * disp_rows % LANES
+                        if shift:
+                            value = pltpu.roll(value, shift, 1)
+                        tile = i * disp_rows // LANES
+                        if filled[tile] is None:
+                            filled[tile] = value
+                        else:
+                            filled[tile] = jnp.where(lane < shift, filled[tile], value)
+                        if shift + disp_rows > LANES:
+                            filled[tile + 1] = value
+                    for tile, value in enumerate(filled):
+                        out_ref[chip, pl.ds(tile * part_rows + first, PACK), :] = (
+                            value * (1.0 / 256.0)
+                        ).astype(jnp.bfloat16)
                     return carry
 
-                lax.fori_loop(0, nodes // 2 // LANES, pack, 0, unroll=4)
+                lax.fori_loop(0, part_rows // PACK, pack, 0)
 
     vmem = pl.BlockSpec(memory_space=pltpu.VMEM)
     smem = pl.BlockSpec(memory_space=pltpu.SMEM)
-    out = jax.ShapeDtypeStruct((cols // 2, nodes // 2, LANES), jnp.bfloat16)
+    out = jax.ShapeDtypeStruct((cols // 2, nodes * disp_rows // LANES, LANES), jnp.bfloat16)
     return pl.pallas_call(
         kernel,
         out_shape=(out, out),
@@ -360,6 +375,49 @@
     )(parity, counts, lists, node_data, centre_data, coefs)
 
 
+def restore(parts, rank, disp_rows):
+    count, packed_rows, _ = parts.shape
+    nodes = rank.shape[1]
+    part_rows = nodes // PARTS
+    tiles = packed_rows // part_rows
+    width = 512
+
+    def kernel(part_ref, rank_ref, out_ref):
+        turned = []
+        for tile in range(tiles):
+            rows_of = slice(tile * part_rows, (tile + 1) * part_rows)
+            total = part_ref[0, rows_of, :].astype(jnp.float32)
+            for i in range(1, count):
+                total = total + part_ref[i, rows_of, :].astype(jnp.float32)
+            turned.append(total.T)
+        turned = jnp.concatenate(turned, axis=0)
+        left = []
+        for i in range(PARTS):
+            value = turned[i * disp_rows : (i + 1) * disp_rows]
+            high = value.astype(jnp.bfloat16)
+            low = (value - high.astype(jnp.float32)).astype(jnp.bfloat16)
+            left.append(jnp.concatenate([high, low], axis=0))
+        sorted_row = lax.broadcasted_iota(jnp.int32, (part_rows, width), 0)
+        for first in range(0, nodes, width):
+            lanes = slice(first, first + width)
+            result = jnp.zeros((2 * disp_rows, width), jnp.float32)
+            for i in range(PARTS):
+                pick = jnp.where(rank_ref[:, lanes] - i * part_rows == sorted_row, 1.0, 0.0)
+                result = result + jnp.dot(
+                    left[i], pick.astype(jnp.bfloat16), preferred_element_type=jnp.float32
+                )
+            out_ref[:, lanes] = result[:disp_rows] + result[disp_rows:]
+
+    vmem = pl.BlockSpec(memory_space=pltpu.VMEM)
+    return pl.pallas_call(
+        kernel,
+        out_shape=jax.ShapeDtypeStruct((disp_rows, nodes), jnp.float32),
+        in_specs=[vmem, vmem],
+        out_specs=vmem,
+        name="restore",
+    )(parts, rank)
+
+
 def per_device(struct_disp, target, inverse, centre_xyz, node_xyz):
     rows = lax.axis_size("row")
     cols = lax.axis_size("col")
@@ -413,14 +471,7 @@
     both = lax.all_to_all(
         both, "col", split_axis=0, concat_axis=0, axis_index_groups=chips, tiled=True
     )
-    summed = jnp.sum(both.astype(jnp.float32), axis=0)
-    ordered = jnp.concatenate([summed[:, :disp_rows], summed[:, 64 : 64 + disp_rows]], axis=0)
-    return lax.dot_general(
-        ordered.astype(jnp.bfloat16),
-        node_pick,
-        (((0,), (1,)), ((), ())),
-        preferred_element_type=jnp.float32,
-    )
+    return restore(both, node_rank[None, :], disp_rows)
 
 
 def solution(mesh):

time: 174 us -> 172 us (0.989)
  Pallas kernels: 33.4 us -> 39.1 us
  matrix products: 26.6 us -> 22.3 us
  blocking collectives: 17.4 us -> 14.7 us
    dot_general x1 -> x0, matrix products: 4.24 us -> none  [per_device(): lax.dot_general(ordered.astype(jnp.bfloat16), node_pick, (((0,), (1,)), (...]
    pallas_call x0 -> x1, Pallas kernels: none -> 3.95 us  [restore(): pl.pallas_call(kernel, out_shape=jax.ShapeDtypeStruct((disp_rows, nodes),...]
    all_to_all x1, blocking collectives: 17.4 us -> 14.7 us  [per_device(): lax.all_to_all(both, 'col', split_axis=0, concat_axis=0, axis_index_group...]
where the time goes in v4:
time: 172 us; the launch traced here: 170 us
  Pallas kernels  39.1 us (23%)
  starting transfers between devices  32 us (19%)
  waiting for transfers between devices  30 us (17%)
  matrix products  22.3 us (13%)
  other arithmetic  18.1 us (11%)
  blocking collectives  14.7 us (9%)
  local copies, waits for them, and re-layouts  13.4 us (8%)
    pallas_call x1, Pallas kernels, interpolate(): pl.pallas_call(kernel, out_shape=(out, out), in_specs=[smem, smem, smem,...  35.2 us
    all_to_all x5, starting transfers between devices, exchange(): return lax.all_to_all(value, axes, split_axis=0, concat_axis=0, tiled=True)  29.3 us
    all_to_all x5, waiting for transfers between devices, exchange(): return lax.all_to_all(value, axes, split_axis=0, concat_axis=0, tiled=True)  27.8 us
    all_to_all x1, blocking collectives, per_device(): lax.all_to_all(both, 'col', split_axis=0, concat_axis=0, axis_index_group...  14.7 us
    dot_general x1, matrix products, per_device(): jnp.dot(partial.astype(jnp.bfloat16), centre_pick, preferred_element_type...  12.1 us
    dot_general x2, matrix products, column_displacements(): lax.dot_general(part[:, :, :disp_rows], place, (((1,), (1,)), ((0,), (0,)...  4.71 us
    convert_element_type x1, other arithmetic, listed_groups(): jnp.where(minor, d[None, :, None], 0).astype(jnp.bfloat16)  4.13 us
    pallas_call x1, Pallas kernels, restore(): pl.pallas_call(kernel, out_shape=jax.ShapeDtypeStruct((disp_rows, nodes),...  3.95 us
  transfers between devices with their start and end apart: 6, of which 6 were waited for; matrix products, arithmetic and copies ran while one was open for 11% of the time, Pallas kernels for 0%

profile of v4, /device:TPU:1, one launch (start us, length us, event | category | flops | bytes accessed | tf_op | source)
XLA Modules:
  0.0 170.3 jit_solution(3482904163587985890)
XLA Ops:
  0.0 0.8 multiply_add_fusion
  0.9 0.8 convert_element_type.114
  2.3 1.2 broadcast_in_dim.173
  3.5 0.8 convert_clamp_fusion
  4.3 0.8 reduce-precision_convert_fusion.1
  5.6 1.7 convert_reduce_fusion.1
  8.8 8.6 %all-to-all-start = ((f32[16,4,256]{2,1,0:T(4,128)}), f32[16,4,256]{2,1,0:T(4,128)S(1)}, u32[]{:S(2)}, u32[]{:S(2)}) async-start(f32[16,4,256]{2,1,0:T(4,128)} %broadcast_in_dim.191), calls=%async_computation | async-start | bytes 131072 | tf_op jit(solution)/shard_map/all_to_all | solution.py:33
  17.9 1.7 convert_reduce_fusion
  19.6 3.0 %fusion.1 = f32[9,2048]{1,0:T(8,128)S(1)} fusion(s32[2048]{0:T(1024)S(1)} %convert_reduce_fusion, bf16[3,2048]{1,0:T(4,128)(2,1)S(1)} %get-tuple-element.60, bf16[3,2048]{1,0:T(4,128)(2,1)S(1)} %get-tuple-element.62, bf16[3,2048]{1,0:T(4,128)(2,1)S(1)} %get-tuple-element.58), kind=kOutput, calls=%fused_computation.5 | convolution fusion | flops 79802368 | bytes 118784 | tf_op jit(solution)/shard_map/dot_general | solution.py:127
  24.7 6.4 %all-to-all-start.1 = ((f32[8,4,2048]{2,1,0:T(4,128)}), f32[8,4,2048]{2,1,0:T(4,128)S(1)}, u32[]{:S(2)}, u32[]{:S(2)}) async-start(f32[8,4,2048]{2,1,0:T(4,128)} %broadcast_in_dim.193), calls=%async_computation.1 | async-start | bytes 524288 | tf_op jit(solution)/shard_map/all_to_all | solution.py:33
  33.4 4.1 %all-to-all-done.1.node_ref = f32[8,4,2048]{2,1,0:T(4,128)S(1)} async-done(((f32[8,4,2048]{2,1,0:T(4,128)}), f32[8,4,2048]{2,1,0:T(4,128)S(1)}, u32[]{:S(2)}, u32[]{:S(2)}) %all-to-all-start.1) | async-done | bytes 262176 | tf_op jit(solution)/shard_map/all_to_all | solution.py:33
  37.5 6.5 %all-to-all-start.2 = ((bf16[128,32,128]{2,1,0:T(8,128)(2,1)}), bf16[128,32,128]{2,1,0:T(8,128)(2,1)S(1)}, u32[]{:S(2)}, u32[]{:S(2)}) async-start(bf16[128,32,128]{2,1,0:T(8,128)(2,1)} %bitcast.1), calls=%async_computation.2 | async-start | bytes 2097152 | tf_op jit(solution)/shard_map/all_to_all | solution.py:33
  44.3 3.2 %add_reduce_fusion = f32[4,2,4,2048]{3,2,1,0:T(4,128)S(1)} fusion(f32[4,4,2,4,2]{3,4,2,1,0:T(2,128)S(1)} %copy.67, f32[2048]{0:T(1024)S(1)} %bitcast.108, f32[2048]{0:T(1024)S(1)} %bitcast.109, f32[4,4,2,4,2]{3,4,2,1,0:T(2,128)S(1)} %copy.65, f32[4,4,2,4,2]{3,4,2,1,0:T(2,128)S(1)} %copy.63, f32[2048]{0:T(1024)S(1)} %bitcast.110, f32[2048]{0:T(1024)S(1)} %bitcast.111, ...), kind=kLoop, calls=%fused_computation.21 | loop fusion | flops 9371648 | bytes 317440 | tf_op jit(solution)/shard_map/reduce_min | solution.py:155
  48.8 4.1 %select_convert_fusion.1 = (bf16[8,2048,128]{2,1,0:T(8,128)(2,1)S(1)}, bf16[8,2048,128]{2,1,0:T(8,128)(2,1)S(1)}) fusion(s32[2048]{0:T(1024)S(1)} %get-tuple-element.95, s32[8,2048]{1,0:T(8,128)S(1)} %add_select_fusion, s32[2048]{0:T(1024)S(1)} %get-tuple-element.94), kind=kLoop, calls=%fused_computation.12 | loop fusion | flops 10485760 | bytes 8470528 | tf_op jit(solution)/shard_map/convert_element_type | solution.py:180
  52.9 1.6 fusion.2
  54.5 8.8 %all-to-all-done.2 = bf16[128,32,128]{2,1,0:T(8,128)(2,1)S(1)} async-done(((bf16[128,32,128]{2,1,0:T(8,128)(2,1)}), bf16[128,32,128]{2,1,0:T(8,128)(2,1)S(1)}, u32[]{:S(2)}, u32[]{:S(2)}) %all-to-all-start.2) | async-done | bytes 1048608 | tf_op jit(solution)/shard_map/all_to_all | solution.py:33
  65.0 1.7 %fusion.124 = (bf16[8,512,48]{2,0,1:T(8,128)(2,1)}, bf16[8,512,48]{2,0,1:T(8,128)(2,1)}) fusion(bf16[8,512,128]{2,0,1:T(8,128)(2,1)S(1)} %bitcast.98), kind=kLoop, calls=%fused_computation.336 | loop fusion | bytes 1572864 | tf_op jit(solution)/shard_map/slice | solution.py:77
  68.2 2.4 %fusion.15 = bf16[8,48,256]{2,1,0:T(8,128)(2,1)S(1)} fusion(bf16[8,512,48]{2,0,1:T(8,128)(2,1)} %get-tuple-element.34, bf16[256]{0:T(256)(128)(2,1)S(1)} %iota_convert_fusion, bf16[8,512]{1,0:T(8,128)(2,1)S(1)} %bitcast.128), kind=kOutput, calls=%fused_computation.25 | convolution fusion | flops 101810176 | bytes 598528 | tf_op jit(solution)/shard_map/dot_general | solution.py:76
  70.6 2.4 %fusion.18 = bf16[8,48,256]{2,1,0:T(8,128)(2,1)S(1)} fusion(bf16[8,512,48]{2,0,1:T(8,128)(2,1)} %get-tuple-element.35, bf16[8,512]{1,0:T(8,128)(2,1)S(1)} %bitcast.127, bf16[256]{0:T(256)(128)(2,1)S(1)} %iota_convert_fusion), kind=kOutput, calls=%fused_computation.26 | convolution fusion | flops 101810176 | bytes 598528 | tf_op jit(solution)/shard_map/dot_general | solution.py:76
  73.0 12.1 %fusion.12 = bf16[48,2048]{1,0:T(8,128)(2,1)S(1)} fusion(s32[2048]{0:T(1024)S(1)} %fusion.68, bf16[48,4096]{1,0:T(8,128)(2,1)S(1)} %bitcast.100, bf16[2048,4096]{1,0:T(8,128)(2,1)} %param.7), kind=kOutput, calls=%fused_computation.19 | convolution fusion | flops 1212350464 | bytes 17375232 | tf_op jit(solution)/shard_map/dot_general | solution.py:459
  85.8 4.3 %all-to-all-start.3 = ((bf16[8,48,256]{2,1,0:T(8,128)(2,1)}), bf16[8,48,256]{2,1,0:T(8,128)(2,1)S(1)}, u32[]{:S(2)}, u32[]{:S(2)}) async-start(bf16[8,48,256]{2,1,0:T(8,128)(2,1)} %bitcast.93), calls=%async_computation.3 | async-start | bytes 393216 | tf_op jit(solution)/shard_map/all_to_all | solution.py:33
  90.1 5.8 %all-to-all-done.3 = bf16[8,48,256]{2,1,0:T(8,128)(2,1)S(1)} async-done(((bf16[8,48,256]{2,1,0:T(8,128)(2,1)}), bf16[8,48,256]{2,1,0:T(8,128)(2,1)S(1)}, u32[]{:S(2)}, u32[]{:S(2)}) %all-to-all-start.3) | async-done | bytes 196640 | tf_op jit(solution)/shard_map/all_to_all | solution.py:33
  96.0 0.8 broadcast_in_dim.202
  96.8 3.6 %all-to-all-start.4 = ((bf16[16,48,256]{2,1,0:T(8,128)(2,1)}), bf16[16,48,256]{2,1,0:T(8,128)(2,1)S(1)}, u32[]{:S(2)}, u32[]{:S(2)}) async-start(bf16[16,48,256]{2,1,0:T(8,128)(2,1)} %broadcast_in_dim.202), calls=%async_computation.4 | async-start | bytes 786432 | tf_op jit(solution)/shard_map/all_to_all | solution.py:33
  101.1 8.5 %all-to-all-done.4.coef_ref = bf16[16,48,256]{2,1,0:T(8,128)(2,1)S(1)} async-done(((bf16[16,48,256]{2,1,0:T(8,128)(2,1)}), bf16[16,48,256]{2,1,0:T(8,128)(2,1)S(1)}, u32[]{:S(2)}, u32[]{:S(2)}) %all-to-all-start.4) | async-done | bytes 393248 | tf_op jit(solution)/shard_map/all_to_all | solution.py:33
  109.5 0.7 copy-done.1
  110.3 35.2 %interpolate.1 = (bf16[4,768,128]{2,1,0:T(8,128)(2,1)}, bf16[4,768,128]{2,1,0:T(8,128)(2,1)}) custom-call(s32[1]{0:T(128)} %bitcast.parity_ref, s32[8]{0:T(128)} %bitcast.132, s32[8,2080]{1,0:T(8,128)} %select_multiply_fusion.list_ref, f32[8,4,2048]{2,1,0:T(4,128)} %copy-done.2, f32[16,4,256]{2,1,0:T(4,128)} %copy-done.3, bf16[16,48,256]{2,1,0:T(8,128)(2,1)} %copy-done.1), custom_call_target="tpu_custom_call" | custom-call | tf_op jit(solution)/shard_map/interpolate/pallas_call | solution.py:358
  145.4 2.7 %collective-permute-start = (bf16[4,768,128]{2,1,0:T(8,128)(2,1)}, bf16[4,768,128]{2,1,0:T(8,128)(2,1)S(1)}, u32[]{:S(2)}, u32[]{:S(2)}) collective-permute-start(bf16[4,768,128]{2,1,0:T(8,128)(2,1)} %get-tuple-element.14), channel_id=1, source_target_pairs={{0,1},{1,0},{2,3},{3,2},{4,5},{5,4},{6,7},{7,6},{8,9},{9,8},{10,11... | collective-permute-start | bytes 2359304 | tf_op jit(solution)/shard_map/ppermute | solution.py:468
  148.1 2.1 %collective-permute-done = bf16[4,768,128]{2,1,0:T(8,128)(2,1)S(1)} collective-permute-done((bf16[4,768,128]{2,1,0:T(8,128)(2,1)}, bf16[4,768,128]{2,1,0:T(8,128)(2,1)S(1)}, u32[]{:S(2)}, u32[]{:S(2)}) %collective-permute-start) | collective-permute-done | bytes 786464 | tf_op jit(solution)/shard_map/ppermute | solution.py:468
  150.3 1.3 add_convert_fusion
  151.6 14.7 %all_to_all.30.part_ref = bf16[4,768,128]{2,1,0:T(8,128)(2,1)} all-to-all(bf16[4,768,128]{2,1,0:T(8,128)(2,1)S(1)} %add_convert_fusion), channel_id=1, replica_groups={{0,2,4,6},{1,3,5,7},{8,10,12,14},{9,11,13,15},{16,18,20,22},{17,19,21,2..., dimensions={0} | all-to-all | bytes 1572864 | tf_op jit(solution)/shard_map/all_to_all | solution.py:471
  166.3 3.9 %restore.1 = f32[48,2048]{1,0:T(8,128)} custom-call(bf16[4,768,128]{2,1,0:T(8,128)(2,1)} %all_to_all.30.part_ref, s32[1,2048]{1,0:T(1,128)} %bitcast.126), custom_call_target="tpu_custom_call" | custom-call | tf_op jit(solution)/shard_map/restore/pallas_call | solution.py:412
  (116 shorter events, 13.3 us)
Async XLA Ops:
  0.0 2.2 %copy-start = (f32[3,32768]{1,0:T(4,128)S(1)}, f32[3,32768]{1,0:T(4,128)}, u32[]{:S(2)}) copy-start(f32[3,32768]{1,0:T(4,128)} %param.8) | copy-start | bytes 1179652
  8.8 15.1 %all-to-all-start = ((f32[16,4,256]{2,1,0:T(4,128)}), f32[16,4,256]{2,1,0:T(4,128)S(1)}, u32[]{:S(2)}, u32[]{:S(2)}) async-start(f32[16,4,256]{2,1,0:T(4,128)} %broadcast_in_dim.191), calls=%async_computation | async-start | bytes 131072 | tf_op jit(solution)/shard_map/all_to_all | solution.py:33
  19.6 17.9 %copy-start.4 = (s32[2048]{0:T(1024)}, s32[2048]{0:T(1024)S(1)}, u32[]{:S(2)}) copy-start(s32[2048]{0:T(1024)S(1)} %convert_reduce_fusion) | copy-start | bytes 24580
  23.9 29.0 %copy-start.3 = (f32[16,4,256]{2,1,0:T(4,128)}, f32[16,4,256]{2,1,0:T(4,128)S(1)}, u32[]{:S(2)}) copy-start(f32[16,4,256]{2,1,0:T(4,128)S(1)} %all-to-all-done.centre_ref) | copy-start | bytes 196612
  24.7 12.9 %all-to-all-start.1 = ((f32[8,4,2048]{2,1,0:T(4,128)}), f32[8,4,2048]{2,1,0:T(4,128)S(1)}, u32[]{:S(2)}, u32[]{:S(2)}) async-start(f32[8,4,2048]{2,1,0:T(4,128)} %broadcast_in_dim.193), calls=%async_computation.1 | async-start | bytes 524288 | tf_op jit(solution)/shard_map/all_to_all | solution.py:33
  37.5 15.4 %copy-start.2 = (f32[8,4,2048]{2,1,0:T(4,128)}, f32[8,4,2048]{2,1,0:T(4,128)S(1)}, u32[]{:S(2)}) copy-start(f32[8,4,2048]{2,1,0:T(4,128)S(1)} %all-to-all-done.1.node_ref) | copy-start | bytes 786436
  37.5 25.8 %all-to-all-start.2 = ((bf16[128,32,128]{2,1,0:T(8,128)(2,1)}), bf16[128,32,128]{2,1,0:T(8,128)(2,1)S(1)}, u32[]{:S(2)}, u32[]{:S(2)}) async-start(bf16[128,32,128]{2,1,0:T(8,128)(2,1)} %bitcast.1), calls=%async_computation.2 | async-start | bytes 2097152 | tf_op jit(solution)/shard_map/all_to_all | solution.py:33
  48.8 51.6 %copy-start.5 = (s32[8,1]{0,1:T(1,128)}, s32[8,1]{0,1:T(1,128)S(1)}, u32[]{:S(2)}) copy-start(s32[8,1]{0,1:T(1,128)S(1)} %copy.91) | copy-start | bytes 100
  85.8 10.1 %all-to-all-start.3 = ((bf16[8,48,256]{2,1,0:T(8,128)(2,1)}), bf16[8,48,256]{2,1,0:T(8,128)(2,1)S(1)}, u32[]{:S(2)}, u32[]{:S(2)}) async-start(bf16[8,48,256]{2,1,0:T(8,128)(2,1)} %bitcast.93), calls=%async_computation.3 | async-start | bytes 393216 | tf_op jit(solution)/shard_map/all_to_all | solution.py:33
  96.8 12.8 %all-to-all-start.4 = ((bf16[16,48,256]{2,1,0:T(8,128)(2,1)}), bf16[16,48,256]{2,1,0:T(8,128)(2,1)S(1)}, u32[]{:S(2)}, u32[]{:S(2)}) async-start(bf16[16,48,256]{2,1,0:T(8,128)(2,1)} %broadcast_in_dim.202), calls=%async_computation.4 | async-start | bytes 786432 | tf_op jit(solution)/shard_map/all_to_all | solution.py:33
  109.5 0.7 copy-start.1
  145.4 4.8 %collective-permute-start = (bf16[4,768,128]{2,1,0:T(8,128)(2,1)}, bf16[4,768,128]{2,1,0:T(8,128)(2,1)S(1)}, u32[]{:S(2)}, u32[]{:S(2)}) collective-permute-start(bf16[4,768,128]{2,1,0:T(8,128)(2,1)} %get-tuple-element.14), channel_id=1, source_target_pairs={{0,1},{1,0},{2,3},{3,2},{4,5},{5,4},{6,7},{7,6},{8,9},{9,8},{10,11... | collective-permute-start | bytes 2359304 | tf_op jit(solution)/shard_map/ppermute | solution.py:468

commit v5 on v4

--- a/solution.py
+++ b/solution.py
@@ -80,8 +80,7 @@
                 preferred_element_type=jnp.float32,
             )
         )
-    summed = jnp.concatenate(halves, axis=0).astype(jnp.bfloat16)
-    return summed.transpose(1, 0, 2).reshape(disp_rows, col_block)
+    return jnp.concatenate(halves, axis=0).astype(jnp.bfloat16)
 
 
 def surface_key(xyz):
@@ -418,6 +417,49 @@
     )(parts, rank)
 
 
+def invert(disp, inverse, slot, cols):
+    spans, disp_rows, width = disp.shape
+    row_block, col_block = inverse.shape
+    piece = row_block // cols
+
+    def kernel(disp_ref, inverse_ref, slot_ref, out_ref, part_ref):
+        step = pl.program_id(0)
+        total = jnp.zeros((disp_rows, piece), jnp.float32)
+        for span in range(spans):
+            total = total + lax.dot_general(
+                disp_ref[span],
+                inverse_ref[:, span * width : (span + 1) * width],
+                (((1,), (1,)), ((), ())),
+                preferred_element_type=jnp.float32,
+            )
+        part_ref[:, pl.ds(pl.multiple_of(step * piece, piece), piece)] = total.astype(jnp.bfloat16)
+
+        @pl.when(step == cols - 1)
+        def _():
+            place = lax.broadcasted_iota(jnp.int32, (piece, row_block), 0)
+            for col in range(cols):
+                pick = jnp.where(slot_ref[...] - col * piece == place, 1.0, 0.0).astype(jnp.bfloat16)
+                moved = lax.dot_general(
+                    part_ref[...], pick, (((1,), (1,)), ((), ())), preferred_element_type=jnp.float32
+                )
+                out_ref[col] = moved.astype(jnp.bfloat16)
+
+    whole = lambda *shape: pl.BlockSpec(shape, lambda i: (0,) * len(shape))
+    return pl.pallas_call(
+        kernel,
+        grid=(cols,),
+        out_shape=jax.ShapeDtypeStruct((cols, disp_rows, piece), jnp.bfloat16),
+        in_specs=[
+            whole(spans, disp_rows, width),
+            pl.BlockSpec((piece, col_block), lambda i: (i, 0)),
+            whole(1, row_block),
+        ],
+        out_specs=whole(cols, disp_rows, piece),
+        scratch_shapes=[pltpu.VMEM((disp_rows, row_block), jnp.bfloat16)],
+        name="invert",
+    )(disp, inverse, slot[None, :])
+
+
 def per_device(struct_disp, target, inverse, centre_xyz, node_xyz):
     rows = lax.axis_size("row")
     cols = lax.axis_size("col")
@@ -437,8 +479,6 @@
     turns = LANES // BLOCK
     place = block // cols
     centre_slot = block % cols * piece + place // turns * LANES + (place + row_index) % turns * BLOCK + rank % BLOCK
-    order = jnp.arange(row_block, dtype=jnp.int32)
-    centre_pick = (centre_slot[:, None] == order[None, :]).astype(jnp.bfloat16)
     piece_order = lax.axis_index("col") * piece + jnp.arange(piece, dtype=jnp.int32)
     piece_pick = (centre_slot[:, None] == piece_order[None, :]).astype(jnp.bfloat16)
     piece_data = with_boxes(pick_columns(own_xyz, piece_pick), BOX)
@@ -453,11 +493,7 @@
     counts, lists = listed_groups(near)
 
     disp_bf = column_displacements(recv, disp_rows, rows, cols, col_block)
-    partial = lax.dot_general(
-        disp_bf, inverse, (((1,), (1,)), ((), ())), preferred_element_type=jnp.float32
-    )
-    partial = jnp.dot(partial.astype(jnp.bfloat16), centre_pick, preferred_element_type=jnp.float32)
-    partial = partial.astype(jnp.bfloat16).reshape(disp_rows, cols, piece).transpose(1, 0, 2)
+    partial = invert(disp_bf, inverse, centre_slot, cols)
     partial = exchange(partial, "col")
     coef = jnp.sum(partial.astype(jnp.float32), axis=0)
     coef = lax.optimization_barrier(coef).astype(jnp.bfloat16)

time: 172 us -> 172 us (level)
  Pallas kernels: 39.1 us -> 53 us
  matrix products: 22.3 us -> 9.28 us
    pallas_call x0 -> x1, Pallas kernels: none -> 13.7 us  [invert(): pl.pallas_call(kernel, grid=(cols,), out_shape=jax.ShapeDtypeStruct((cols...]
    dot_general x1 -> x0, matrix products: 12.1 us -> none  [per_device(): jnp.dot(partial.astype(jnp.bfloat16), centre_pick, preferred_element_type...]
  transfers between devices with their start and end apart: 6 -> 6, of which waited for: 6 -> 5; matrix products, arithmetic and copies ran while one was open for 11% -> 12% of each run, Pallas kernels for 0% -> 0%
where the time goes in v5:
time: 172 us; the launch traced here: 170 us
  Pallas kernels  53 us (31%)
  starting transfers between devices  32.7 us (19%)
  waiting for transfers between devices  29.3 us (17%)
  other arithmetic  18.1 us (11%)
  blocking collectives  14.7 us (9%)
  local copies, waits for them, and re-layouts  12.7 us (7%)
  matrix products  9.28 us (5%)
    pallas_call x1, Pallas kernels, interpolate(): pl.pallas_call(kernel, out_shape=(out, out), in_specs=[smem, smem, smem,...  35.3 us
    all_to_all x5, starting transfers between devices, exchange(): return lax.all_to_all(value, axes, split_axis=0, concat_axis=0, tiled=True)  30 us
    all_to_all x5, waiting for transfers between devices, exchange(): return lax.all_to_all(value, axes, split_axis=0, concat_axis=0, tiled=True)  27.2 us
    all_to_all x1, blocking collectives, per_device(): lax.all_to_all(both, 'col', split_axis=0, concat_axis=0, axis_index_group...  14.7 us
    pallas_call x1, Pallas kernels, invert(): pl.pallas_call(kernel, grid=(cols,), out_shape=jax.ShapeDtypeStruct((cols...  13.7 us
    convert_element_type x1, other arithmetic, listed_groups(): jnp.where(minor, d[None, :, None], 0).astype(jnp.bfloat16)  4.13 us
    pallas_call x1, Pallas kernels, restore(): pl.pallas_call(kernel, out_shape=jax.ShapeDtypeStruct((disp_rows, nodes),...  3.95 us
    dot_general x2, matrix products, column_displacements(): lax.dot_general(part[:, :, :disp_rows], place, (((1,), (1,)), ((0,), (0,)...  3.77 us
  transfers between devices with their start and end apart: 6, of which 5 were waited for; matrix products, arithmetic and copies ran while one was open for 12% of the time, Pallas kernels for 0%

profile of v5, /device:TPU:1, one launch (start us, length us, event | category | flops | bytes accessed | tf_op | source)
XLA Modules:
  0.0 170.4 jit_solution(14596960997328562314)
XLA Ops:
  0.0 0.8 multiply_add_fusion
  0.9 0.8 convert_element_type.107
  2.3 1.2 broadcast_in_dim.172
  4.1 1.7 convert_reduce_fusion.1
  7.3 8.6 %all-to-all-start = ((f32[16,4,256]{2,1,0:T(4,128)}), f32[16,4,256]{2,1,0:T(4,128)S(1)}, u32[]{:S(2)}, u32[]{:S(2)}) async-start(f32[16,4,256]{2,1,0:T(4,128)} %broadcast_in_dim.190), calls=%async_computation | async-start | bytes 131072 | tf_op jit(solution)/shard_map/all_to_all | solution.py:33
  16.0 0.8 fusion.62.slot_ref
  17.2 1.7 convert_reduce_fusion
  18.9 3.0 %fusion = f32[9,2048]{1,0:T(8,128)S(1)} fusion(s32[2048]{0:T(1024)S(1)} %convert_reduce_fusion, bf16[3,2048]{1,0:T(4,128)(2,1)S(1)} %get-tuple-element.60, bf16[3,2048]{1,0:T(4,128)(2,1)S(1)} %get-tuple-element.62, bf16[3,2048]{1,0:T(4,128)(2,1)S(1)} %get-tuple-element.58), kind=kOutput, calls=%fused_computation.3 | convolution fusion | flops 79802368 | bytes 118784 | tf_op jit(solution)/shard_map/dot_general | solution.py:126
  23.3 6.3 %all-to-all-start.1 = ((f32[8,4,2048]{2,1,0:T(4,128)}), f32[8,4,2048]{2,1,0:T(4,128)S(1)}, u32[]{:S(2)}, u32[]{:S(2)}) async-start(f32[8,4,2048]{2,1,0:T(4,128)} %broadcast_in_dim.192), calls=%async_computation.1 | async-start | bytes 524288 | tf_op jit(solution)/shard_map/all_to_all | solution.py:33
  31.9 4.1 %all-to-all-done.1.node_ref = f32[8,4,2048]{2,1,0:T(4,128)S(1)} async-done(((f32[8,4,2048]{2,1,0:T(4,128)}), f32[8,4,2048]{2,1,0:T(4,128)S(1)}, u32[]{:S(2)}, u32[]{:S(2)}) %all-to-all-start.1) | async-done | bytes 262176 | tf_op jit(solution)/shard_map/all_to_all | solution.py:33
  36.0 7.3 %all-to-all-start.2 = ((bf16[128,32,128]{2,1,0:T(8,128)(2,1)}), bf16[128,32,128]{2,1,0:T(8,128)(2,1)S(1)}, u32[]{:S(2)}, u32[]{:S(2)}) async-start(bf16[128,32,128]{2,1,0:T(8,128)(2,1)} %bitcast.1), calls=%async_computation.2 | async-start | bytes 2097152 | tf_op jit(solution)/shard_map/all_to_all | solution.py:33
  43.5 3.2 %add_reduce_fusion = f32[4,2,4,2048]{3,2,1,0:T(4,128)S(1)} fusion(f32[4,4,2,4,2]{3,4,2,1,0:T(2,128)S(1)} %copy.64, f32[2048]{0:T(1024)S(1)} %bitcast.94, f32[2048]{0:T(1024)S(1)} %bitcast.95, f32[4,4,2,4,2]{3,4,2,1,0:T(2,128)S(1)} %copy.62, f32[4,4,2,4,2]{3,4,2,1,0:T(2,128)S(1)} %copy.60, f32[2048]{0:T(1024)S(1)} %bitcast.96, f32[2048]{0:T(1024)S(1)} %bitcast.97, ...), kind=kLoop, calls=%fused_computation.16 | loop fusion | flops 9371648 | bytes 317440 | tf_op jit(solution)/shard_map/reduce_min | solution.py:154
  48.1 4.1 %select_convert_fusion.1 = (bf16[8,2048,128]{2,1,0:T(8,128)(2,1)S(1)}, bf16[8,2048,128]{2,1,0:T(8,128)(2,1)S(1)}) fusion(s32[2048]{0:T(1024)S(1)} %get-tuple-element.95, s32[8,2048]{1,0:T(8,128)S(1)} %add_select_fusion, s32[2048]{0:T(1024)S(1)} %get-tuple-element.94), kind=kLoop, calls=%fused_computation.9 | loop fusion | flops 10485760 | bytes 8470528 | tf_op jit(solution)/shard_map/convert_element_type | solution.py:179
  52.2 1.6 fusion.1
  53.8 8.8 %all-to-all-done.2 = bf16[128,32,128]{2,1,0:T(8,128)(2,1)S(1)} async-done(((bf16[128,32,128]{2,1,0:T(8,128)(2,1)}), bf16[128,32,128]{2,1,0:T(8,128)(2,1)S(1)}, u32[]{:S(2)}, u32[]{:S(2)}) %all-to-all-start.2) | async-done | bytes 1048608 | tf_op jit(solution)/shard_map/all_to_all | solution.py:33
  64.3 1.7 %fusion.127 = (bf16[8,512,48]{2,0,1:T(8,128)(2,1)}, bf16[8,512,48]{2,0,1:T(8,128)(2,1)}) fusion(bf16[8,512,128]{2,0,1:T(8,128)(2,1)S(1)} %bitcast.86), kind=kLoop, calls=%fused_computation.353 | loop fusion | bytes 1572864 | tf_op jit(solution)/shard_map/slice | solution.py:77
  67.5 2.4 %fusion.12 = bf16[8,48,256]{2,1,0:T(8,128)(2,1)S(1)} fusion(bf16[8,512,48]{2,0,1:T(8,128)(2,1)} %get-tuple-element.34, bf16[256]{0:T(256)(128)(2,1)S(1)} %iota_convert_fusion, bf16[8,512]{1,0:T(8,128)(2,1)S(1)} %bitcast.115), kind=kOutput, calls=%fused_computation.20 | convolution fusion | flops 101810176 | bytes 598528 | tf_op jit(solution)/shard_map/dot_general | solution.py:76
  69.9 1.4 fusion.15
  71.3 0.8 pad_maximum_fusion.disp_ref
  72.1 13.7 %invert.1 = bf16[8,48,256]{2,1,0:T(8,128)(2,1)} custom-call(bf16[16,48,256]{2,1,0:T(8,128)(2,1)} %pad_maximum_fusion.disp_ref, bf16[2048,4096]{1,0:T(8,128)(2,1)} %inverse_ref.1, s32[1,2048]{1,0:T(1,128)} %fusion.62.slot_ref), custom_call_target="tpu_custom_call" | custom-call | tf_op jit(solution)/shard_map/invert/pallas_call | solution.py:448
  85.7 4.3 %all-to-all-start.3 = ((bf16[8,48,256]{2,1,0:T(8,128)(2,1)}), bf16[8,48,256]{2,1,0:T(8,128)(2,1)S(1)}, u32[]{:S(2)}, u32[]{:S(2)}) async-start(bf16[8,48,256]{2,1,0:T(8,128)(2,1)} %invert.1), calls=%async_computation.3 | async-start | bytes 393216 | tf_op jit(solution)/shard_map/all_to_all | solution.py:33
  90.0 5.8 %all-to-all-done.3 = bf16[8,48,256]{2,1,0:T(8,128)(2,1)S(1)} async-done(((bf16[8,48,256]{2,1,0:T(8,128)(2,1)}), bf16[8,48,256]{2,1,0:T(8,128)(2,1)S(1)}, u32[]{:S(2)}, u32[]{:S(2)}) %all-to-all-start.3) | async-done | bytes 196640 | tf_op jit(solution)/shard_map/all_to_all | solution.py:33
  95.9 0.8 broadcast_in_dim.201
  96.7 3.6 %all-to-all-start.4 = ((bf16[16,48,256]{2,1,0:T(8,128)(2,1)}), bf16[16,48,256]{2,1,0:T(8,128)(2,1)S(1)}, u32[]{:S(2)}, u32[]{:S(2)}) async-start(bf16[16,48,256]{2,1,0:T(8,128)(2,1)} %broadcast_in_dim.201), calls=%async_computation.4 | async-start | bytes 786432 | tf_op jit(solution)/shard_map/all_to_all | solution.py:33
  101.0 8.5 %all-to-all-done.4.coef_ref = bf16[16,48,256]{2,1,0:T(8,128)(2,1)S(1)} async-done(((bf16[16,48,256]{2,1,0:T(8,128)(2,1)}), bf16[16,48,256]{2,1,0:T(8,128)(2,1)S(1)}, u32[]{:S(2)}, u32[]{:S(2)}) %all-to-all-start.4) | async-done | bytes 393248 | tf_op jit(solution)/shard_map/all_to_all | solution.py:33
  109.4 0.7 copy-done.1
  110.2 35.3 %interpolate.1 = (bf16[4,768,128]{2,1,0:T(8,128)(2,1)}, bf16[4,768,128]{2,1,0:T(8,128)(2,1)}) custom-call(s32[1]{0:T(128)} %bitcast.parity_ref, s32[8]{0:T(128)} %bitcast.119, s32[8,2080]{1,0:T(8,128)} %select_multiply_fusion.list_ref, f32[8,4,2048]{2,1,0:T(4,128)} %copy-done.2, f32[16,4,256]{2,1,0:T(4,128)} %copy-done.4, bf16[16,48,256]{2,1,0:T(8,128)(2,1)} %copy-done.1), custom_call_target="tpu_custom_call" | custom-call | tf_op jit(solution)/shard_map/interpolate/pallas_call | solution.py:357
  145.5 2.7 %collective-permute-start = (bf16[4,768,128]{2,1,0:T(8,128)(2,1)}, bf16[4,768,128]{2,1,0:T(8,128)(2,1)S(1)}, u32[]{:S(2)}, u32[]{:S(2)}) collective-permute-start(bf16[4,768,128]{2,1,0:T(8,128)(2,1)} %get-tuple-element.14), channel_id=1, source_target_pairs={{0,1},{1,0},{2,3},{3,2},{4,5},{5,4},{6,7},{7,6},{8,9},{9,8},{10,11... | collective-permute-start | bytes 2359304 | tf_op jit(solution)/shard_map/ppermute | solution.py:504
  148.2 2.1 %collective-permute-done = bf16[4,768,128]{2,1,0:T(8,128)(2,1)S(1)} collective-permute-done((bf16[4,768,128]{2,1,0:T(8,128)(2,1)}, bf16[4,768,128]{2,1,0:T(8,128)(2,1)S(1)}, u32[]{:S(2)}, u32[]{:S(2)}) %collective-permute-start) | collective-permute-done | bytes 786464 | tf_op jit(solution)/shard_map/ppermute | solution.py:504
  150.3 1.3 add_convert_fusion
  151.7 14.7 %all_to_all.30.part_ref = bf16[4,768,128]{2,1,0:T(8,128)(2,1)} all-to-all(bf16[4,768,128]{2,1,0:T(8,128)(2,1)S(1)} %add_convert_fusion), channel_id=1, replica_groups={{0,2,4,6},{1,3,5,7},{8,10,12,14},{9,11,13,15},{16,18,20,22},{17,19,21,2..., dimensions={0} | all-to-all | bytes 1572864 | tf_op jit(solution)/shard_map/all_to_all | solution.py:507
  166.4 3.9 %restore.1 = f32[48,2048]{1,0:T(8,128)} custom-call(bf16[4,768,128]{2,1,0:T(8,128)(2,1)} %all_to_all.30.part_ref, s32[1,2048]{1,0:T(1,128)} %bitcast.113), custom_call_target="tpu_custom_call" | custom-call | tf_op jit(solution)/shard_map/restore/pallas_call | solution.py:411
  (119 shorter events, 12.0 us)
Async XLA Ops:
  0.0 2.2 %copy-start = (f32[3,32768]{1,0:T(4,128)S(1)}, f32[3,32768]{1,0:T(4,128)}, u32[]{:S(2)}) copy-start(f32[3,32768]{1,0:T(4,128)} %param.8) | copy-start | bytes 1179652
  0.0 3.5 %copy-start.5 = (f32[3,2048]{1,0:T(4,128)S(1)}, f32[3,2048]{1,0:T(4,128)}, u32[]{:S(2)}) copy-start(f32[3,2048]{1,0:T(4,128)} %param.9) | copy-start | bytes 73732
  7.3 15.2 %all-to-all-start = ((f32[16,4,256]{2,1,0:T(4,128)}), f32[16,4,256]{2,1,0:T(4,128)S(1)}, u32[]{:S(2)}, u32[]{:S(2)}) async-start(f32[16,4,256]{2,1,0:T(4,128)} %broadcast_in_dim.190), calls=%async_computation | async-start | bytes 131072 | tf_op jit(solution)/shard_map/all_to_all | solution.py:33
  18.9 3.0 %copy-start.6 = (s32[2048]{0:T(1024)}, s32[2048]{0:T(1024)S(1)}, u32[]{:S(2)}) copy-start(s32[2048]{0:T(1024)S(1)} %convert_reduce_fusion) | copy-start | bytes 24580
  22.5 21.0 %copy-start.4 = (f32[16,4,256]{2,1,0:T(4,128)}, f32[16,4,256]{2,1,0:T(4,128)S(1)}, u32[]{:S(2)}) copy-start(f32[16,4,256]{2,1,0:T(4,128)S(1)} %all-to-all-done.centre_ref) | copy-start | bytes 196612
  23.3 12.7 %all-to-all-start.1 = ((f32[8,4,2048]{2,1,0:T(4,128)}), f32[8,4,2048]{2,1,0:T(4,128)S(1)}, u32[]{:S(2)}, u32[]{:S(2)}) async-start(f32[8,4,2048]{2,1,0:T(4,128)} %broadcast_in_dim.192), calls=%async_computation.1 | async-start | bytes 524288 | tf_op jit(solution)/shard_map/all_to_all | solution.py:33
  36.0 11.0 %copy-start.2 = (f32[8,4,2048]{2,1,0:T(4,128)}, f32[8,4,2048]{2,1,0:T(4,128)S(1)}, u32[]{:S(2)}) copy-start(f32[8,4,2048]{2,1,0:T(4,128)S(1)} %all-to-all-done.1.node_ref) | copy-start | bytes 786436
  36.0 26.6 %all-to-all-start.2 = ((bf16[128,32,128]{2,1,0:T(8,128)(2,1)}), bf16[128,32,128]{2,1,0:T(8,128)(2,1)S(1)}, u32[]{:S(2)}, u32[]{:S(2)}) async-start(bf16[128,32,128]{2,1,0:T(8,128)(2,1)} %bitcast.1), calls=%async_computation.2 | async-start | bytes 2097152 | tf_op jit(solution)/shard_map/all_to_all | solution.py:33
  48.1 52.2 %copy-start.7 = (s32[8,1]{0,1:T(1,128)}, s32[8,1]{0,1:T(1,128)S(1)}, u32[]{:S(2)}) copy-start(s32[8,1]{0,1:T(1,128)S(1)} %copy.84) | copy-start | bytes 100
  66.8 3.1 %copy-start.3 = (bf16[8,512,48]{2,0,1:T(8,128)(2,1)S(1)}, bf16[8,512,48]{2,0,1:T(8,128)(2,1)}, u32[]{:S(2)}) copy-start(bf16[8,512,48]{2,0,1:T(8,128)(2,1)} %get-tuple-element.35) | copy-start | bytes 1179652
  85.7 10.1 %all-to-all-start.3 = ((bf16[8,48,256]{2,1,0:T(8,128)(2,1)}), bf16[8,48,256]{2,1,0:T(8,128)(2,1)S(1)}, u32[]{:S(2)}, u32[]{:S(2)}) async-start(bf16[8,48,256]{2,1,0:T(8,128)(2,1)} %invert.1), calls=%async_computation.3 | async-start | bytes 393216 | tf_op jit(solution)/shard_map/all_to_all | solution.py:33
  96.7 12.8 %all-to-all-start.4 = ((bf16[16,48,256]{2,1,0:T(8,128)(2,1)}), bf16[16,48,256]{2,1,0:T(8,128)(2,1)S(1)}, u32[]{:S(2)}, u32[]{:S(2)}) async-start(bf16[16,48,256]{2,1,0:T(8,128)(2,1)} %broadcast_in_dim.201), calls=%async_computation.4 | async-start | bytes 786432 | tf_op jit(solution)/shard_map/all_to_all | solution.py:33
  109.4 0.7 copy-start.1
  145.5 4.8 %collective-permute-start = (bf16[4,768,128]{2,1,0:T(8,128)(2,1)}, bf16[4,768,128]{2,1,0:T(8,128)(2,1)S(1)}, u32[]{:S(2)}, u32[]{:S(2)}) collective-permute-start(bf16[4,768,128]{2,1,0:T(8,128)(2,1)} %get-tuple-element.14), channel_id=1, source_target_pairs={{0,1},{1,0},{2,3},{3,2},{4,5},{5,4},{6,7},{7,6},{8,9},{9,8},{10,11... | collective-permute-start | bytes 2359304 | tf_op jit(solution)/shard_map/ppermute | solution.py:504

commit v6 on v4

--- a/solution.py
+++ b/solution.py
@@ -63,25 +63,38 @@
     return jnp.broadcast_to(packed[None], (rows, cols, half, 128)).reshape(rows * cols, half, 128)
 
 
-def column_displacements(recv, disp_rows, rows, cols, col_block):
-    owner_block = col_block // rows
-    recv = recv.reshape(rows * cols, rows // 2, CAP, 128).transpose(1, 0, 2, 3)
-    recv = recv.reshape(rows // 2, rows * cols * CAP, 128)
-    columns = jnp.arange(owner_block, dtype=jnp.int32).astype(jnp.bfloat16)
-    halves = []
-    for side in range(2):
-        part = recv[:, :, side * 64 : side * 64 + 64]
-        place = (part[:, :, disp_rows : disp_rows + 1] == columns[None, None, :]).astype(jnp.bfloat16)
-        halves.append(
-            lax.dot_general(
-                part[:, :, :disp_rows],
-                place,
-                (((1,), (1,)), ((0,), (0,))),
-                preferred_element_type=jnp.float32,
-            )
-        )
-    summed = jnp.concatenate(halves, axis=0).astype(jnp.bfloat16)
-    return summed.transpose(1, 0, 2).reshape(disp_rows, col_block)
+def column_displacements(recv, disp_rows, rows, owner_block):
+    sources, half, _ = recv.shape
+    pair = 2 * CAP
+    count = sources * pair
+
+    def kernel(recv_ref, out_ref):
+        column = lax.broadcasted_iota(jnp.int32, (count, 2 * owner_block), 1).astype(jnp.float32)
+        row = lax.broadcasted_iota(jnp.int32, (count, 1), 0)
+        second = jnp.where(row % pair >= CAP, float(owner_block), 0.0)
+        for first in range(0, half, 2 * pair):
+            block = recv_ref[:, first : first + 2 * pair, :].astype(jnp.float32)
+            for part in range(2):
+                entries = block[:, part * pair : (part + 1) * pair, :].reshape(count, LANES)
+                turned = entries.T.astype(jnp.bfloat16)
+                for side in range(2):
+                    lane = side * (LANES // 2)
+                    offset = entries[:, lane + disp_rows : lane + disp_rows + 1] + second
+                    place = jnp.where(offset == column, 1.0, 0.0).astype(jnp.bfloat16)
+                    moved = jnp.dot(
+                        turned[lane : lane + disp_rows], place, preferred_element_type=jnp.float32
+                    ).astype(jnp.bfloat16)
+                    owner = side * (rows // 2) + (first // pair + part) * 2
+                    out_ref[:, owner * owner_block : (owner + 2) * owner_block] = moved
+
+    vmem = pl.BlockSpec(memory_space=pltpu.VMEM)
+    return pl.pallas_call(
+        kernel,
+        out_shape=jax.ShapeDtypeStruct((disp_rows, rows * owner_block), jnp.bfloat16),
+        in_specs=[vmem],
+        out_specs=vmem,
+        name="unpack",
+    )(recv)
 
 
 def surface_key(xyz):
@@ -452,7 +465,7 @@
     near = near_groups(centre_data, node_data)
     counts, lists = listed_groups(near)
 
-    disp_bf = column_displacements(recv, disp_rows, rows, cols, col_block)
+    disp_bf = column_displacements(recv, disp_rows, rows, col_block // rows)
     partial = lax.dot_general(
         disp_bf, inverse, (((1,), (1,)), ((), ())), preferred_element_type=jnp.float32
     )

time: 172 us -> 167 us (0.971)
  matrix products: 22.3 us -> 17.4 us
  Pallas kernels: 39.1 us -> 43.1 us
  local copies, waits for them, and re-layouts: 13.4 us -> 9.46 us
    dot_general x2 -> x0, matrix products: 4.71 us -> none  [column_displacements(): lax.dot_general(part[:, :, :disp_rows], place, (((1,), (1,)), ((0,), (0,)...]
    pallas_call x0 -> x1, Pallas kernels: none -> 3.95 us  [column_displacements(): pl.pallas_call(kernel, out_shape=jax.ShapeDtypeStruct((disp_rows, rows *...]
    slice x4 -> x0, local copies, waits for them, and re-layouts: 3.8 us -> none  [the longest x3 2.07 us: column_displacements(): part[:, :, disp_rows:disp_rows + 1] == columns[None, None, :]]
where the time goes in v6:
time: 167 us; the launch traced here: 165 us
  Pallas kernels  43.1 us (26%)
  starting transfers between devices  32 us (19%)
  waiting for transfers between devices  30 us (18%)
  other arithmetic  18 us (11%)
  matrix products  17.4 us (10%)
  blocking collectives  14.7 us (9%)
  local copies, waits for them, and re-layouts  9.46 us (6%)
    pallas_call x1, Pallas kernels, interpolate(): pl.pallas_call(kernel, out_shape=(out, out), in_specs=[smem, smem, smem,...  35.2 us
    all_to_all x5, starting transfers between devices, exchange(): return lax.all_to_all(value, axes, split_axis=0, concat_axis=0, tiled=True)  29.3 us
    all_to_all x5, waiting for transfers between devices, exchange(): return lax.all_to_all(value, axes, split_axis=0, concat_axis=0, tiled=True)  27.9 us
    all_to_all x1, blocking collectives, per_device(): lax.all_to_all(both, 'col', split_axis=0, concat_axis=0, axis_index_group...  14.7 us
    dot_general x1, matrix products, per_device(): jnp.dot(partial.astype(jnp.bfloat16), centre_pick, preferred_element_type...  11.9 us
    convert_element_type x1, other arithmetic, listed_groups(): jnp.where(minor, d[None, :, None], 0).astype(jnp.bfloat16)  4.13 us
    pallas_call x1, Pallas kernels, column_displacements(): pl.pallas_call(kernel, out_shape=jax.ShapeDtypeStruct((disp_rows, rows *...  3.95 us
    pallas_call x1, Pallas kernels, restore(): pl.pallas_call(kernel, out_shape=jax.ShapeDtypeStruct((disp_rows, nodes),...  3.95 us
  transfers between devices with their start and end apart: 6, of which 6 were waited for; matrix products, arithmetic and copies ran while one was open for 11% of the time, Pallas kernels for 0%

profile of v6, /device:TPU:1, one launch (start us, length us, event | category | flops | bytes accessed | tf_op | source)
XLA Modules:
  0.0 165.2 jit_solution(1938151430909877081)
XLA Ops:
  0.0 0.8 multiply_add_fusion
  0.9 0.8 convert_element_type.102
  2.3 1.2 broadcast_in_dim.171
  3.5 0.8 convert_clamp_fusion
  4.3 0.8 reduce-precision_convert_fusion.1
  5.6 1.7 %convert_reduce_fusion.1 = s32[2048]{0:T(1024)S(1)} fusion(s32[2048]{0:T(1024)S(1)} %bitcast.113, s32[2048]{0:T(1024)S(1)} %iota_add_fusion.3), kind=kLoop, calls=%fused_computation.3 | loop fusion | flops 12580864 | bytes 24576 | tf_op jit(solution)/shard_map/reduce_sum | solution.py:132
  8.8 8.6 %all-to-all-start = ((f32[16,4,256]{2,1,0:T(4,128)}), f32[16,4,256]{2,1,0:T(4,128)S(1)}, u32[]{:S(2)}, u32[]{:S(2)}) async-start(f32[16,4,256]{2,1,0:T(4,128)} %broadcast_in_dim.189), calls=%async_computation | async-start | bytes 131072 | tf_op jit(solution)/shard_map/all_to_all | solution.py:33
  17.9 1.7 %convert_reduce_fusion = s32[2048]{0:T(1024)S(1)} fusion(s32[2048]{0:T(1024)S(1)} %bitcast.114, s32[2048]{0:T(1024)S(1)} %iota_add_fusion.1), kind=kLoop, calls=%fused_computation.2 | loop fusion | flops 12580864 | bytes 24576 | tf_op jit(solution)/shard_map/reduce_sum | solution.py:132
  19.6 3.0 %fusion.1 = f32[9,2048]{1,0:T(8,128)S(1)} fusion(s32[2048]{0:T(1024)S(1)} %convert_reduce_fusion, bf16[3,2048]{1,0:T(4,128)(2,1)S(1)} %get-tuple-element.56, bf16[3,2048]{1,0:T(4,128)(2,1)S(1)} %get-tuple-element.58, bf16[3,2048]{1,0:T(4,128)(2,1)S(1)} %get-tuple-element.54), kind=kOutput, calls=%fused_computation.5 | convolution fusion | flops 79802368 | bytes 118784 | tf_op jit(solution)/shard_map/dot_general | solution.py:140
  23.9 0.7 broadcast_in_dim.191
  24.7 6.4 %all-to-all-start.1 = ((f32[8,4,2048]{2,1,0:T(4,128)}), f32[8,4,2048]{2,1,0:T(4,128)S(1)}, u32[]{:S(2)}, u32[]{:S(2)}) async-start(f32[8,4,2048]{2,1,0:T(4,128)} %broadcast_in_dim.191), calls=%async_computation.1 | async-start | bytes 524288 | tf_op jit(solution)/shard_map/all_to_all | solution.py:33
  33.4 4.1 %all-to-all-done.1.node_ref = f32[8,4,2048]{2,1,0:T(4,128)S(1)} async-done(((f32[8,4,2048]{2,1,0:T(4,128)}), f32[8,4,2048]{2,1,0:T(4,128)S(1)}, u32[]{:S(2)}, u32[]{:S(2)}) %all-to-all-start.1) | async-done | bytes 262176 | tf_op jit(solution)/shard_map/all_to_all | solution.py:33
  37.5 6.5 %all-to-all-start.2 = ((bf16[128,32,128]{2,1,0:T(8,128)(2,1)}), bf16[128,32,128]{2,1,0:T(8,128)(2,1)S(1)}, u32[]{:S(2)}, u32[]{:S(2)}) async-start(bf16[128,32,128]{2,1,0:T(8,128)(2,1)} %bitcast.1), calls=%async_computation.2 | async-start | bytes 2097152 | tf_op jit(solution)/shard_map/all_to_all | solution.py:33
  44.2 3.2 %add_reduce_fusion = f32[4,2,4,2048]{3,2,1,0:T(4,128)S(1)} fusion(f32[4,4,2,4,2]{3,4,2,1,0:T(2,128)S(1)} %copy.54, f32[2048]{0:T(1024)S(1)} %bitcast.94, f32[2048]{0:T(1024)S(1)} %bitcast.95, f32[4,4,2,4,2]{3,4,2,1,0:T(2,128)S(1)} %copy.52, f32[4,4,2,4,2]{3,4,2,1,0:T(2,128)S(1)} %copy.50, f32[2048]{0:T(1024)S(1)} %bitcast.96, f32[2048]{0:T(1024)S(1)} %bitcast.97, ...), kind=kLoop, calls=%fused_computation.17 | loop fusion | flops 9371648 | bytes 317440 | tf_op jit(solution)/shard_map/reduce_min | solution.py:168
  48.8 4.1 %select_convert_fusion.1 = (bf16[8,2048,128]{2,1,0:T(8,128)(2,1)S(1)}, bf16[8,2048,128]{2,1,0:T(8,128)(2,1)S(1)}) fusion(s32[2048]{0:T(1024)S(1)} %get-tuple-element.91, s32[8,2048]{1,0:T(8,128)S(1)} %add_select_fusion, s32[2048]{0:T(1024)S(1)} %get-tuple-element.90), kind=kLoop, calls=%fused_computation.12 | loop fusion | flops 10485760 | bytes 8470528 | tf_op jit(solution)/shard_map/convert_element_type | solution.py:193
  52.9 1.6 fusion.2
  54.5 8.8 %all-to-all-done.2.recv_ref = bf16[128,32,128]{2,1,0:T(8,128)(2,1)S(1)} async-done(((bf16[128,32,128]{2,1,0:T(8,128)(2,1)}), bf16[128,32,128]{2,1,0:T(8,128)(2,1)S(1)}, u32[]{:S(2)}, u32[]{:S(2)}) %all-to-all-start.2) | async-done | bytes 1048608 | tf_op jit(solution)/shard_map/all_to_all | solution.py:33
  63.3 1.0 copy-done.1
  64.3 4.0 %unpack.1 = bf16[48,4096]{1,0:T(8,128)(2,1)} custom-call(bf16[128,32,128]{2,1,0:T(8,128)(2,1)} %copy-done.1), custom_call_target="tpu_custom_call" | custom-call | tf_op jit(solution)/shard_map/unpack/pallas_call | solution.py:91
  68.2 11.9 %fusion.8 = bf16[48,2048]{1,0:T(8,128)(2,1)S(1)} fusion(s32[2048]{0:T(1024)S(1)} %fusion.52, bf16[48,4096]{1,0:T(8,128)(2,1)} %unpack.1, bf16[2048,4096]{1,0:T(8,128)(2,1)} %param.7), kind=kOutput, calls=%fused_computation.15 | convolution fusion | flops 1212350464 | bytes 17375232 | tf_op jit(solution)/shard_map/dot_general | solution.py:472
  80.8 4.3 %all-to-all-start.3 = ((bf16[8,48,256]{2,1,0:T(8,128)(2,1)}), bf16[8,48,256]{2,1,0:T(8,128)(2,1)S(1)}, u32[]{:S(2)}, u32[]{:S(2)}) async-start(bf16[8,48,256]{2,1,0:T(8,128)(2,1)} %bitcast.83), calls=%async_computation.3 | async-start | bytes 393216 | tf_op jit(solution)/shard_map/all_to_all | solution.py:33
  85.1 5.8 %all-to-all-done.3 = bf16[8,48,256]{2,1,0:T(8,128)(2,1)S(1)} async-done(((bf16[8,48,256]{2,1,0:T(8,128)(2,1)}), bf16[8,48,256]{2,1,0:T(8,128)(2,1)S(1)}, u32[]{:S(2)}, u32[]{:S(2)}) %all-to-all-start.3) | async-done | bytes 196640 | tf_op jit(solution)/shard_map/all_to_all | solution.py:33
  91.0 0.8 broadcast_in_dim.200
  91.8 3.6 %all-to-all-start.4 = ((bf16[16,48,256]{2,1,0:T(8,128)(2,1)}), bf16[16,48,256]{2,1,0:T(8,128)(2,1)S(1)}, u32[]{:S(2)}, u32[]{:S(2)}) async-start(bf16[16,48,256]{2,1,0:T(8,128)(2,1)} %broadcast_in_dim.200), calls=%async_computation.4 | async-start | bytes 786432 | tf_op jit(solution)/shard_map/all_to_all | solution.py:33
  96.1 8.5 %all-to-all-done.4.coef_ref = bf16[16,48,256]{2,1,0:T(8,128)(2,1)S(1)} async-done(((bf16[16,48,256]{2,1,0:T(8,128)(2,1)}), bf16[16,48,256]{2,1,0:T(8,128)(2,1)S(1)}, u32[]{:S(2)}, u32[]{:S(2)}) %all-to-all-start.4) | async-done | bytes 393248 | tf_op jit(solution)/shard_map/all_to_all | solution.py:33
  104.5 0.7 copy-done.2
  105.3 35.2 %interpolate.1 = (bf16[4,768,128]{2,1,0:T(8,128)(2,1)}, bf16[4,768,128]{2,1,0:T(8,128)(2,1)}) custom-call(s32[1]{0:T(128)} %bitcast.parity_ref, s32[8]{0:T(128)} %bitcast.116, s32[8,2080]{1,0:T(8,128)} %select_multiply_fusion.list_ref, f32[8,4,2048]{2,1,0:T(4,128)} %copy-done.3, f32[16,4,256]{2,1,0:T(4,128)} %copy-done.4, bf16[16,48,256]{2,1,0:T(8,128)(2,1)} %copy-done.2), custom_call_target="tpu_custom_call" | custom-call | tf_op jit(solution)/shard_map/interpolate/pallas_call | solution.py:371
  140.5 2.7 %collective-permute-start = (bf16[4,768,128]{2,1,0:T(8,128)(2,1)}, bf16[4,768,128]{2,1,0:T(8,128)(2,1)S(1)}, u32[]{:S(2)}, u32[]{:S(2)}) collective-permute-start(bf16[4,768,128]{2,1,0:T(8,128)(2,1)} %get-tuple-element.14), channel_id=1, source_target_pairs={{0,1},{1,0},{2,3},{3,2},{4,5},{5,4},{6,7},{7,6},{8,9},{9,8},{10,11... | collective-permute-start | bytes 2359304 | tf_op jit(solution)/shard_map/ppermute | solution.py:481
  143.1 2.1 %collective-permute-done = bf16[4,768,128]{2,1,0:T(8,128)(2,1)S(1)} collective-permute-done((bf16[4,768,128]{2,1,0:T(8,128)(2,1)}, bf16[4,768,128]{2,1,0:T(8,128)(2,1)S(1)}, u32[]{:S(2)}, u32[]{:S(2)}) %collective-permute-start) | collective-permute-done | bytes 786464 | tf_op jit(solution)/shard_map/ppermute | solution.py:481
  145.2 1.3 add_convert_fusion
  146.6 14.7 %all_to_all.30.part_ref = bf16[4,768,128]{2,1,0:T(8,128)(2,1)} all-to-all(bf16[4,768,128]{2,1,0:T(8,128)(2,1)S(1)} %add_convert_fusion), channel_id=1, replica_groups={{0,2,4,6},{1,3,5,7},{8,10,12,14},{9,11,13,15},{16,18,20,22},{17,19,21,2..., dimensions={0} | all-to-all | bytes 1572864 | tf_op jit(solution)/shard_map/all_to_all | solution.py:484
  161.3 3.9 %restore.1 = f32[48,2048]{1,0:T(8,128)} custom-call(bf16[4,768,128]{2,1,0:T(8,128)(2,1)} %all_to_all.30.part_ref, s32[1,2048]{1,0:T(1,128)} %bitcast.112), custom_call_target="tpu_custom_call" | custom-call | tf_op jit(solution)/shard_map/restore/pallas_call | solution.py:425
  (108 shorter events, 9.4 us)
Async XLA Ops:
  0.0 2.2 %copy-start = (f32[3,32768]{1,0:T(4,128)S(1)}, f32[3,32768]{1,0:T(4,128)}, u32[]{:S(2)}) copy-start(f32[3,32768]{1,0:T(4,128)} %param.8) | copy-start | bytes 1179652
  8.8 15.1 %all-to-all-start = ((f32[16,4,256]{2,1,0:T(4,128)}), f32[16,4,256]{2,1,0:T(4,128)S(1)}, u32[]{:S(2)}, u32[]{:S(2)}) async-start(f32[16,4,256]{2,1,0:T(4,128)} %broadcast_in_dim.189), calls=%async_computation | async-start | bytes 131072 | tf_op jit(solution)/shard_map/all_to_all | solution.py:33
  19.6 17.9 %copy-start.5 = (s32[2048]{0:T(1024)}, s32[2048]{0:T(1024)S(1)}, u32[]{:S(2)}) copy-start(s32[2048]{0:T(1024)S(1)} %convert_reduce_fusion) | copy-start | bytes 24580
  23.9 29.0 %copy-start.4 = (f32[16,4,256]{2,1,0:T(4,128)}, f32[16,4,256]{2,1,0:T(4,128)S(1)}, u32[]{:S(2)}) copy-start(f32[16,4,256]{2,1,0:T(4,128)S(1)} %all-to-all-done.centre_ref) | copy-start | bytes 196612
  24.7 12.9 %all-to-all-start.1 = ((f32[8,4,2048]{2,1,0:T(4,128)}), f32[8,4,2048]{2,1,0:T(4,128)S(1)}, u32[]{:S(2)}, u32[]{:S(2)}) async-start(f32[8,4,2048]{2,1,0:T(4,128)} %broadcast_in_dim.191), calls=%async_computation.1 | async-start | bytes 524288 | tf_op jit(solution)/shard_map/all_to_all | solution.py:33
  37.5 15.4 %copy-start.3 = (f32[8,4,2048]{2,1,0:T(4,128)}, f32[8,4,2048]{2,1,0:T(4,128)S(1)}, u32[]{:S(2)}) copy-start(f32[8,4,2048]{2,1,0:T(4,128)S(1)} %all-to-all-done.1.node_ref) | copy-start | bytes 786436
  37.5 25.8 %all-to-all-start.2 = ((bf16[128,32,128]{2,1,0:T(8,128)(2,1)}), bf16[128,32,128]{2,1,0:T(8,128)(2,1)S(1)}, u32[]{:S(2)}, u32[]{:S(2)}) async-start(bf16[128,32,128]{2,1,0:T(8,128)(2,1)} %bitcast.1), calls=%async_computation.2 | async-start | bytes 2097152 | tf_op jit(solution)/shard_map/all_to_all | solution.py:33
  48.8 46.6 %copy-start.6 = (s32[8,1]{0,1:T(1,128)}, s32[8,1]{0,1:T(1,128)S(1)}, u32[]{:S(2)}) copy-start(s32[8,1]{0,1:T(1,128)S(1)} %copy.68) | copy-start | bytes 100
  63.3 1.0 copy-start.1
  80.8 10.1 %all-to-all-start.3 = ((bf16[8,48,256]{2,1,0:T(8,128)(2,1)}), bf16[8,48,256]{2,1,0:T(8,128)(2,1)S(1)}, u32[]{:S(2)}, u32[]{:S(2)}) async-start(bf16[8,48,256]{2,1,0:T(8,128)(2,1)} %bitcast.83), calls=%async_computation.3 | async-start | bytes 393216 | tf_op jit(solution)/shard_map/all_to_all | solution.py:33
  91.8 12.8 %all-to-all-start.4 = ((bf16[16,48,256]{2,1,0:T(8,128)(2,1)}), bf16[16,48,256]{2,1,0:T(8,128)(2,1)S(1)}, u32[]{:S(2)}, u32[]{:S(2)}) async-start(bf16[16,48,256]{2,1,0:T(8,128)(2,1)} %broadcast_in_dim.200), calls=%async_computation.4 | async-start | bytes 786432 | tf_op jit(solution)/shard_map/all_to_all | solution.py:33
  104.5 0.7 copy-start.2
  140.5 4.8 %collective-permute-start = (bf16[4,768,128]{2,1,0:T(8,128)(2,1)}, bf16[4,768,128]{2,1,0:T(8,128)(2,1)S(1)}, u32[]{:S(2)}, u32[]{:S(2)}) collective-permute-start(bf16[4,768,128]{2,1,0:T(8,128)(2,1)} %get-tuple-element.14), channel_id=1, source_target_pairs={{0,1},{1,0},{2,3},{3,2},{4,5},{5,4},{6,7},{7,6},{8,9},{9,8},{10,11... | collective-permute-start | bytes 2359304 | tf_op jit(solution)/shard_map/ppermute | solution.py:481

commit v7 on v6

--- a/solution.py
+++ b/solution.py
@@ -18,7 +18,7 @@
 BLOCK = 32
 BOX = 16
 PARTS = 8
-PACK = 64
+PACK = 256
 FACES = (
     (1, 0, (0, 0, 0), 0),
     (2, 0, (1, 0, 0), 0),
@@ -244,7 +244,7 @@
                 acc_ref[pl.ds(col * nodes + first, LANES), :] = jnp.zeros((LANES, LANES), jnp.float32)
                 return carry
 
-            lax.fori_loop(0, nodes // LANES, prepare, 0, unroll=4)
+            lax.fori_loop(0, nodes // LANES, prepare, 0, unroll=16)
 
         lane = lax.broadcasted_iota(jnp.int32, (1, LANES), 1)
         segment = lane // BLOCK
@@ -318,9 +318,11 @@
                 preferred_element_type=jnp.float32,
             )
             places = [pl.ds(pl.multiple_of(start, GROUP), GROUP) for start in starts(place)]
-            before = [acc_ref[rows_of, :disp_rows] for rows_of in places]
-            for i, rows_of in enumerate(places):
-                acc_ref[rows_of, :disp_rows] = before[i] + part[i * GROUP : (i + 1) * GROUP]
+            for first in range(0, BATCH, 8):
+                before = [acc_ref[places[i], :disp_rows] for i in range(first, first + 8)]
+                for i in range(first, first + 8):
+                    moved = part[i * GROUP : (i + 1) * GROUP]
+                    acc_ref[places[i], :disp_rows] = before[i - first] + moved
 
         spread(1, spread_0)
 

time: 167 us -> 161 us (0.964)
  Pallas kernels: 43.1 us -> 37.8 us
    pallas_call x1, Pallas kernels: 35.2 us -> 29.9 us  [interpolate(): pl.pallas_call(kernel, out_shape=(out, out), in_specs=[smem, smem, smem,...]
  transfers between devices with their start and end apart: 6 -> 6, of which waited for: 6 -> 6; matrix products, arithmetic and copies ran while one was open for 11% -> 12% of each run, Pallas kernels for 0% -> 0%
where the time goes in v7:
time: 161 us; the launch traced here: 160 us
  Pallas kernels  37.8 us (23%)
  starting transfers between devices  31.9 us (20%)
  waiting for transfers between devices  30 us (19%)
  other arithmetic  18 us (11%)
  matrix products  17.4 us (11%)
  blocking collectives  14.6 us (9%)
  local copies, waits for them, and re-layouts  9.46 us (6%)
    pallas_call x1, Pallas kernels, interpolate(): pl.pallas_call(kernel, out_shape=(out, out), in_specs=[smem, smem, smem,...  29.9 us
    all_to_all x5, starting transfers between devices, exchange(): return lax.all_to_all(value, axes, split_axis=0, concat_axis=0, tiled=True)  29.3 us
    all_to_all x5, waiting for transfers between devices, exchange(): return lax.all_to_all(value, axes, split_axis=0, concat_axis=0, tiled=True)  27.9 us
    all_to_all x1, blocking collectives, per_device(): lax.all_to_all(both, 'col', split_axis=0, concat_axis=0, axis_index_group...  14.6 us
    dot_general x1, matrix products, per_device(): jnp.dot(partial.astype(jnp.bfloat16), centre_pick, preferred_element_type...  11.9 us
    convert_element_type x1, other arithmetic, listed_groups(): jnp.where(minor, d[None, :, None], 0).astype(jnp.bfloat16)  4.13 us
    pallas_call x1, Pallas kernels, column_displacements(): pl.pallas_call(kernel, out_shape=jax.ShapeDtypeStruct((disp_rows, rows *...  3.95 us
    pallas_call x1, Pallas kernels, restore(): pl.pallas_call(kernel, out_shape=jax.ShapeDtypeStruct((disp_rows, nodes),...  3.95 us
  transfers between devices with their start and end apart: 6, of which 6 were waited for; matrix products, arithmetic and copies ran while one was open for 12% of the time, Pallas kernels for 0%

profile of v7, /device:TPU:1, one launch (start us, length us, event | category | flops | bytes accessed | tf_op | source)
XLA Modules:
  0.0 159.8 jit_solution(12943919173731840551)
XLA Ops:
  0.0 0.8 multiply_add_fusion
  0.9 0.8 convert_element_type.102
  2.3 1.2 broadcast_in_dim.171
  3.5 0.8 convert_clamp_fusion
  4.3 0.8 reduce-precision_convert_fusion.1
  5.6 1.7 %convert_reduce_fusion.1 = s32[2048]{0:T(1024)S(1)} fusion(s32[2048]{0:T(1024)S(1)} %bitcast.113, s32[2048]{0:T(1024)S(1)} %iota_add_fusion.3), kind=kLoop, calls=%fused_computation.3 | loop fusion | flops 12580864 | bytes 24576 | tf_op jit(solution)/shard_map/reduce_sum | solution.py:132
  8.8 8.6 %all-to-all-start = ((f32[16,4,256]{2,1,0:T(4,128)}), f32[16,4,256]{2,1,0:T(4,128)S(1)}, u32[]{:S(2)}, u32[]{:S(2)}) async-start(f32[16,4,256]{2,1,0:T(4,128)} %broadcast_in_dim.189), calls=%async_computation | async-start | bytes 131072 | tf_op jit(solution)/shard_map/all_to_all | solution.py:33
  17.9 1.7 %convert_reduce_fusion = s32[2048]{0:T(1024)S(1)} fusion(s32[2048]{0:T(1024)S(1)} %bitcast.114, s32[2048]{0:T(1024)S(1)} %iota_add_fusion.1), kind=kLoop, calls=%fused_computation.2 | loop fusion | flops 12580864 | bytes 24576 | tf_op jit(solution)/shard_map/reduce_sum | solution.py:132
  19.6 3.0 %fusion.1 = f32[9,2048]{1,0:T(8,128)S(1)} fusion(s32[2048]{0:T(1024)S(1)} %convert_reduce_fusion, bf16[3,2048]{1,0:T(4,128)(2,1)S(1)} %get-tuple-element.56, bf16[3,2048]{1,0:T(4,128)(2,1)S(1)} %get-tuple-element.58, bf16[3,2048]{1,0:T(4,128)(2,1)S(1)} %get-tuple-element.54), kind=kOutput, calls=%fused_computation.5 | convolution fusion | flops 79802368 | bytes 118784 | tf_op jit(solution)/shard_map/dot_general | solution.py:140
  23.9 0.7 broadcast_in_dim.191
  24.7 6.4 %all-to-all-start.1 = ((f32[8,4,2048]{2,1,0:T(4,128)}), f32[8,4,2048]{2,1,0:T(4,128)S(1)}, u32[]{:S(2)}, u32[]{:S(2)}) async-start(f32[8,4,2048]{2,1,0:T(4,128)} %broadcast_in_dim.191), calls=%async_computation.1 | async-start | bytes 524288 | tf_op jit(solution)/shard_map/all_to_all | solution.py:33
  33.4 4.1 %all-to-all-done.1.node_ref = f32[8,4,2048]{2,1,0:T(4,128)S(1)} async-done(((f32[8,4,2048]{2,1,0:T(4,128)}), f32[8,4,2048]{2,1,0:T(4,128)S(1)}, u32[]{:S(2)}, u32[]{:S(2)}) %all-to-all-start.1) | async-done | bytes 262176 | tf_op jit(solution)/shard_map/all_to_all | solution.py:33
  37.5 6.5 %all-to-all-start.2 = ((bf16[128,32,128]{2,1,0:T(8,128)(2,1)}), bf16[128,32,128]{2,1,0:T(8,128)(2,1)S(1)}, u32[]{:S(2)}, u32[]{:S(2)}) async-start(bf16[128,32,128]{2,1,0:T(8,128)(2,1)} %bitcast.1), calls=%async_computation.2 | async-start | bytes 2097152 | tf_op jit(solution)/shard_map/all_to_all | solution.py:33
  44.2 3.2 %add_reduce_fusion = f32[4,2,4,2048]{3,2,1,0:T(4,128)S(1)} fusion(f32[4,4,2,4,2]{3,4,2,1,0:T(2,128)S(1)} %copy.54, f32[2048]{0:T(1024)S(1)} %bitcast.94, f32[2048]{0:T(1024)S(1)} %bitcast.95, f32[4,4,2,4,2]{3,4,2,1,0:T(2,128)S(1)} %copy.52, f32[4,4,2,4,2]{3,4,2,1,0:T(2,128)S(1)} %copy.50, f32[2048]{0:T(1024)S(1)} %bitcast.96, f32[2048]{0:T(1024)S(1)} %bitcast.97, ...), kind=kLoop, calls=%fused_computation.17 | loop fusion | flops 9371648 | bytes 317440 | tf_op jit(solution)/shard_map/reduce_min | solution.py:168
  48.8 4.1 %select_convert_fusion.1 = (bf16[8,2048,128]{2,1,0:T(8,128)(2,1)S(1)}, bf16[8,2048,128]{2,1,0:T(8,128)(2,1)S(1)}) fusion(s32[2048]{0:T(1024)S(1)} %get-tuple-element.91, s32[8,2048]{1,0:T(8,128)S(1)} %add_select_fusion, s32[2048]{0:T(1024)S(1)} %get-tuple-element.90), kind=kLoop, calls=%fused_computation.12 | loop fusion | flops 10485760 | bytes 8470528 | tf_op jit(solution)/shard_map/convert_element_type | solution.py:193
  52.9 1.6 %fusion.2 = f32[8,16,256]{2,1,0:T(8,128)S(1)} fusion(bf16[8,2048,128]{2,1,0:T(8,128)(2,1)S(1)} %get-tuple-element.39, bf16[8,2048,128]{2,1,0:T(8,128)(2,1)S(1)} %get-tuple-element.38, s32[8,2048]{1,0:T(8,128)S(1)} %get-tuple-element.19, pred[8,2048]{1,0:T(8,128)(4,1)S(1)} %get-tuple-element.20), kind=kOutput, calls=%fused_computation.6 | convolution fusion | flops 151519232 | bytes 8601600 | tf_op jit(solution)/shard_map/dot_general | solution.py:194
  54.5 8.8 %all-to-all-done.2.recv_ref = bf16[128,32,128]{2,1,0:T(8,128)(2,1)S(1)} async-done(((bf16[128,32,128]{2,1,0:T(8,128)(2,1)}), bf16[128,32,128]{2,1,0:T(8,128)(2,1)S(1)}, u32[]{:S(2)}, u32[]{:S(2)}) %all-to-all-start.2) | async-done | bytes 1048608 | tf_op jit(solution)/shard_map/all_to_all | solution.py:33
  63.3 1.0 copy-done.1
  64.3 4.0 %unpack.1 = bf16[48,4096]{1,0:T(8,128)(2,1)} custom-call(bf16[128,32,128]{2,1,0:T(8,128)(2,1)} %copy-done.1), custom_call_target="tpu_custom_call" | custom-call | tf_op jit(solution)/shard_map/unpack/pallas_call | solution.py:91
  68.2 11.9 %fusion.8 = bf16[48,2048]{1,0:T(8,128)(2,1)S(1)} fusion(s32[2048]{0:T(1024)S(1)} %fusion.52, bf16[48,4096]{1,0:T(8,128)(2,1)} %unpack.1, bf16[2048,4096]{1,0:T(8,128)(2,1)} %param.7), kind=kOutput, calls=%fused_computation.15 | convolution fusion | flops 1212350464 | bytes 17375232 | tf_op jit(solution)/shard_map/dot_general | solution.py:474
  80.8 4.3 %all-to-all-start.3 = ((bf16[8,48,256]{2,1,0:T(8,128)(2,1)}), bf16[8,48,256]{2,1,0:T(8,128)(2,1)S(1)}, u32[]{:S(2)}, u32[]{:S(2)}) async-start(bf16[8,48,256]{2,1,0:T(8,128)(2,1)} %bitcast.83), calls=%async_computation.3 | async-start | bytes 393216 | tf_op jit(solution)/shard_map/all_to_all | solution.py:33
  85.1 5.8 %all-to-all-done.3 = bf16[8,48,256]{2,1,0:T(8,128)(2,1)S(1)} async-done(((bf16[8,48,256]{2,1,0:T(8,128)(2,1)}), bf16[8,48,256]{2,1,0:T(8,128)(2,1)S(1)}, u32[]{:S(2)}, u32[]{:S(2)}) %all-to-all-start.3) | async-done | bytes 196640 | tf_op jit(solution)/shard_map/all_to_all | solution.py:33
  91.0 0.8 broadcast_in_dim.200
  91.8 3.6 %all-to-all-start.4 = ((bf16[16,48,256]{2,1,0:T(8,128)(2,1)}), bf16[16,48,256]{2,1,0:T(8,128)(2,1)S(1)}, u32[]{:S(2)}, u32[]{:S(2)}) async-start(bf16[16,48,256]{2,1,0:T(8,128)(2,1)} %broadcast_in_dim.200), calls=%async_computation.4 | async-start | bytes 786432 | tf_op jit(solution)/shard_map/all_to_all | solution.py:33
  96.1 8.5 %all-to-all-done.4.coef_ref = bf16[16,48,256]{2,1,0:T(8,128)(2,1)S(1)} async-done(((bf16[16,48,256]{2,1,0:T(8,128)(2,1)}), bf16[16,48,256]{2,1,0:T(8,128)(2,1)S(1)}, u32[]{:S(2)}, u32[]{:S(2)}) %all-to-all-start.4) | async-done | bytes 393248 | tf_op jit(solution)/shard_map/all_to_all | solution.py:33
  104.5 0.7 copy-done.2
  105.3 29.9 %interpolate.1 = (bf16[4,768,128]{2,1,0:T(8,128)(2,1)}, bf16[4,768,128]{2,1,0:T(8,128)(2,1)}) custom-call(s32[1]{0:T(128)} %bitcast.parity_ref, s32[8]{0:T(128)} %bitcast.116, s32[8,2080]{1,0:T(8,128)} %select_multiply_fusion.list_ref, f32[8,4,2048]{2,1,0:T(4,128)} %copy-done.3, f32[16,4,256]{2,1,0:T(4,128)} %copy-done.4, bf16[16,48,256]{2,1,0:T(8,128)(2,1)} %copy-done.2), custom_call_target="tpu_custom_call" | custom-call | tf_op jit(solution)/shard_map/interpolate/pallas_call | solution.py:373
  135.2 2.6 %collective-permute-start = (bf16[4,768,128]{2,1,0:T(8,128)(2,1)}, bf16[4,768,128]{2,1,0:T(8,128)(2,1)S(1)}, u32[]{:S(2)}, u32[]{:S(2)}) collective-permute-start(bf16[4,768,128]{2,1,0:T(8,128)(2,1)} %get-tuple-element.14), channel_id=1, source_target_pairs={{0,1},{1,0},{2,3},{3,2},{4,5},{5,4},{6,7},{7,6},{8,9},{9,8},{10,11... | collective-permute-start | bytes 2359304 | tf_op jit(solution)/shard_map/ppermute | solution.py:483
  137.8 2.1 %collective-permute-done = bf16[4,768,128]{2,1,0:T(8,128)(2,1)S(1)} collective-permute-done((bf16[4,768,128]{2,1,0:T(8,128)(2,1)}, bf16[4,768,128]{2,1,0:T(8,128)(2,1)S(1)}, u32[]{:S(2)}, u32[]{:S(2)}) %collective-permute-start) | collective-permute-done | bytes 786464 | tf_op jit(solution)/shard_map/ppermute | solution.py:483
  139.9 1.3 add_convert_fusion
  141.3 14.6 %all_to_all.30.part_ref = bf16[4,768,128]{2,1,0:T(8,128)(2,1)} all-to-all(bf16[4,768,128]{2,1,0:T(8,128)(2,1)S(1)} %add_convert_fusion), channel_id=1, replica_groups={{0,2,4,6},{1,3,5,7},{8,10,12,14},{9,11,13,15},{16,18,20,22},{17,19,21,2..., dimensions={0} | all-to-all | bytes 1572864 | tf_op jit(solution)/shard_map/all_to_all | solution.py:486
  155.8 3.9 %restore.1 = f32[48,2048]{1,0:T(8,128)} custom-call(bf16[4,768,128]{2,1,0:T(8,128)(2,1)} %all_to_all.30.part_ref, s32[1,2048]{1,0:T(1,128)} %bitcast.112), custom_call_target="tpu_custom_call" | custom-call | tf_op jit(solution)/shard_map/restore/pallas_call | solution.py:427
  (108 shorter events, 9.4 us)
Async XLA Ops:
  0.0 2.2 %copy-start = (f32[3,32768]{1,0:T(4,128)S(1)}, f32[3,32768]{1,0:T(4,128)}, u32[]{:S(2)}) copy-start(f32[3,32768]{1,0:T(4,128)} %param.8) | copy-start | bytes 1179652
  8.8 15.1 %all-to-all-start = ((f32[16,4,256]{2,1,0:T(4,128)}), f32[16,4,256]{2,1,0:T(4,128)S(1)}, u32[]{:S(2)}, u32[]{:S(2)}) async-start(f32[16,4,256]{2,1,0:T(4,128)} %broadcast_in_dim.189), calls=%async_computation | async-start | bytes 131072 | tf_op jit(solution)/shard_map/all_to_all | solution.py:33
  19.6 17.9 %copy-start.5 = (s32[2048]{0:T(1024)}, s32[2048]{0:T(1024)S(1)}, u32[]{:S(2)}) copy-start(s32[2048]{0:T(1024)S(1)} %convert_reduce_fusion) | copy-start | bytes 24580
  23.9 29.0 %copy-start.4 = (f32[16,4,256]{2,1,0:T(4,128)}, f32[16,4,256]{2,1,0:T(4,128)S(1)}, u32[]{:S(2)}) copy-start(f32[16,4,256]{2,1,0:T(4,128)S(1)} %all-to-all-done.centre_ref) | copy-start | bytes 196612
  24.7 12.9 %all-to-all-start.1 = ((f32[8,4,2048]{2,1,0:T(4,128)}), f32[8,4,2048]{2,1,0:T(4,128)S(1)}, u32[]{:S(2)}, u32[]{:S(2)}) async-start(f32[8,4,2048]{2,1,0:T(4,128)} %broadcast_in_dim.191), calls=%async_computation.1 | async-start | bytes 524288 | tf_op jit(solution)/shard_map/all_to_all | solution.py:33
  37.5 15.4 %copy-start.3 = (f32[8,4,2048]{2,1,0:T(4,128)}, f32[8,4,2048]{2,1,0:T(4,128)S(1)}, u32[]{:S(2)}) copy-start(f32[8,4,2048]{2,1,0:T(4,128)S(1)} %all-to-all-done.1.node_ref) | copy-start | bytes 786436
  37.5 25.8 %all-to-all-start.2 = ((bf16[128,32,128]{2,1,0:T(8,128)(2,1)}), bf16[128,32,128]{2,1,0:T(8,128)(2,1)S(1)}, u32[]{:S(2)}, u32[]{:S(2)}) async-start(bf16[128,32,128]{2,1,0:T(8,128)(2,1)} %bitcast.1), calls=%async_computation.2 | async-start | bytes 2097152 | tf_op jit(solution)/shard_map/all_to_all | solution.py:33
  48.8 46.6 %copy-start.6 = (s32[8,1]{0,1:T(1,128)}, s32[8,1]{0,1:T(1,128)S(1)}, u32[]{:S(2)}) copy-start(s32[8,1]{0,1:T(1,128)S(1)} %copy.68) | copy-start | bytes 100
  63.3 1.0 copy-start.1
  80.8 10.1 %all-to-all-start.3 = ((bf16[8,48,256]{2,1,0:T(8,128)(2,1)}), bf16[8,48,256]{2,1,0:T(8,128)(2,1)S(1)}, u32[]{:S(2)}, u32[]{:S(2)}) async-start(bf16[8,48,256]{2,1,0:T(8,128)(2,1)} %bitcast.83), calls=%async_computation.3 | async-start | bytes 393216 | tf_op jit(solution)/shard_map/all_to_all | solution.py:33
  91.8 12.8 %all-to-all-start.4 = ((bf16[16,48,256]{2,1,0:T(8,128)(2,1)}), bf16[16,48,256]{2,1,0:T(8,128)(2,1)S(1)}, u32[]{:S(2)}, u32[]{:S(2)}) async-start(bf16[16,48,256]{2,1,0:T(8,128)(2,1)} %broadcast_in_dim.200), calls=%async_computation.4 | async-start | bytes 786432 | tf_op jit(solution)/shard_map/all_to_all | solution.py:33
  104.5 0.7 copy-start.2
  135.2 4.7 %collective-permute-start = (bf16[4,768,128]{2,1,0:T(8,128)(2,1)}, bf16[4,768,128]{2,1,0:T(8,128)(2,1)S(1)}, u32[]{:S(2)}, u32[]{:S(2)}) collective-permute-start(bf16[4,768,128]{2,1,0:T(8,128)(2,1)} %get-tuple-element.14), channel_id=1, source_target_pairs={{0,1},{1,0},{2,3},{3,2},{4,5},{5,4},{6,7},{7,6},{8,9},{9,8},{10,11... | collective-permute-start | bytes 2359304 | tf_op jit(solution)/shard_map/ppermute | solution.py:483
